TPU v7x, 256 devices: a whole 4x4x8 slice. The times are simulated.
256 devices in a mesh: crop: 2 (over y_hi), rows: 16 (over y_lo, x, core), hid: 8 (over z).
Axes of the slice: x: 4, y: 4 (y_hi: 2, y_lo: 2; y = y_hi * 2 + y_lo), z: 8, core: 2. Of those that a mesh axis runs over, the one named last changes fastest.
Arguments:
- tokens: bfloat16 [2, 32, 64, 4096], P('crop', 'rows', None, 'hid'), may hold values from -6 to 6
- cotangent: bfloat16 [2, 32, 64, 4096], P('crop', 'rows', None, 'hid'), may hold values from -6 to 6
- weight_in: bfloat16 [256, 64, 5, 256], P('rows', 'hid'), may hold values from -0.15625 to 0.15625
- weight_out: bfloat16 [256, 64, 5, 256], P('rows', 'hid'), may hold values from -0.078125 to 0.078125
- mix_kernel: float32 [9, 16384], P(None, 'hid'), may hold values from -4 to 4
- block_rows: int32 [64, 5], P('hid'), may hold values from 0 to 15, as said below
Outputs:
- grad_tokens: bfloat16 [2, 32, 64, 4096], P('crop', 'rows', None, 'hid')
- grad_w_in: float32 [256, 64, 5, 256], P(('crop', 'rows'), 'hid')
- grad_w_out: float32 [256, 64, 5, 256], P(('crop', 'rows'), 'hid')
- grad_kernel: float32 [9, 16384], P(None, 'hid')
Inputs may be any that keep to these rules, and one draw needn't show every extreme that they name: In each block column c, block_rows[c, 0] is a label L and block_rows[c, k] for k >= 1 is L with bit k - 1 flipped, so the 5 entries of a column differ; every value is the label of equally many block columns.
All inputs are finite; a program needn't handle non-finite values.
Results may differ from a plain program's by a relative error of at most 0.019.
Values may be sent and summed in bfloat16 or wider, within the bound.
No kernel may reach another device: no remote copies, remote signals or barrier semaphores. Data moves between devices by JAX's collectives and lax.ppermute only.
A program may use at most 128 MiB of HBM per device.

v0:
```python
import jax
import jax.numpy as jnp
from jax import lax
from jax.sharding import PartitionSpec as P

root_two_pi = 0.7978845608
cubic_coef = 0.044715
loss_scale = 0.03125


def padded(shard, sides, width):
    for axis, dim in sides:
        devices, length = (lax.axis_size(axis), shard.shape[dim])
        up = [(i, (i + 1) % devices) for i in range(devices - 1)]
        down = [(j, i) for i, j in up]
        last = lax.slice_in_dim(shard, length - width, length, axis=dim)
        initial = lax.slice_in_dim(shard, 0, width, axis=dim)
        before = lax.ppermute(last, axis, up)
        after = lax.ppermute(initial, axis, down)
        shard = jnp.concatenate([before, shard, after], axis=dim)
    return shard


def gelu_pair(preact):
    inner = root_two_pi * (preact + cubic_coef * preact * preact * preact)
    tanh_val = jnp.tanh(inner)
    gelu_out = 0.5 * preact * (1.0 + tanh_val)
    slopes = 0.5 * (1.0 + tanh_val) + 0.5 * preact * (1.0 - tanh_val * tanh_val) * root_two_pi * (
        1.0 + 3.0 * cubic_coef * preact * preact
    )
    return (gelu_out, slopes)


def on_device(tokens, cotangent, weight_in, weight_out, mix_kernel, block_rows):
    in_panel, out_panel = (
        lax.all_gather(weight_in, "rows", axis=0, tiled=True),
        lax.all_gather(weight_out, "rows", axis=0, tiled=True),
    )
    tok_full, cot_full = (
        lax.all_gather(tokens, "hid", axis=3, tiled=True),
        lax.all_gather(cotangent, "hid", axis=3, tiled=True),
    )
    crop_count, height, grid_width, depth_all = tok_full.shape
    tok_count = crop_count * height * grid_width
    block_size = in_panel.shape[0]
    col_count = in_panel.shape[1]
    nnz_count = in_panel.shape[2]
    block_count = depth_all // block_size
    hidden_local = col_count * block_size
    flat_rows = block_rows.reshape(-1)
    in_select = jnp.take(
        tok_full.reshape(tok_count, block_count, block_size), flat_rows, axis=1
    ).reshape(tok_count, col_count, nnz_count, block_size)
    grad_select = jnp.take(
        cot_full.reshape(tok_count, block_count, block_size), flat_rows, axis=1
    ).reshape(tok_count, col_count, nnz_count, block_size)
    pre_act = jnp.einsum("tckb,bcke->tce", in_select, in_panel, preferred_element_type=jnp.float32)
    gelu_out, slopes = gelu_pair(pre_act)
    active = gelu_out.astype(jnp.bfloat16).reshape(crop_count, height, grid_width, hidden_local)
    act_rim = padded(active, (("rows", 1),), 1)
    mix_grad = (
        jnp.einsum("tckd,fckd->tcf", grad_select, out_panel, preferred_element_type=jnp.float32)
        .astype(jnp.bfloat16)
        .reshape(crop_count, height, grid_width, hidden_local)
    )
    grad_rim = padded(mix_grad, (("rows", 1),), 1)
    act_pad = jnp.pad(act_rim.astype(jnp.float32), ((0, 0), (0, 0), (1, 1), (0, 0)))
    grad_pad = jnp.pad(grad_rim.astype(jnp.float32), ((0, 0), (0, 0), (1, 1), (0, 0)))
    grad_grid = mix_grad.astype(jnp.float32)
    mix_sum = jnp.zeros((crop_count, height, grid_width, hidden_local), jnp.float32)
    act_grad = jnp.zeros((crop_count, height, grid_width, hidden_local), jnp.float32)
    kern_terms = []
    for row_off in range(3):
        for col_off in range(3):
            tap = mix_kernel[3 * row_off + col_off]
            shifted = act_pad[:, row_off : row_off + height, col_off : col_off + grid_width]
            mix_sum = mix_sum + tap * shifted
            act_grad = (
                act_grad
                + tap
                * grad_pad[
                    :, 2 - row_off : 2 - row_off + height, 2 - col_off : 2 - col_off + grid_width
                ]
            )
            kern_terms.append(jnp.sum(shifted * grad_grid, axis=(0, 1, 2)))
    kern_local = jnp.stack(kern_terms, axis=0) * loss_scale
    mix_out = mix_sum.astype(jnp.bfloat16).reshape(tok_count, col_count, block_size)
    pre_grad = (act_grad.reshape(tok_count, col_count, block_size) * slopes).astype(jnp.bfloat16)
    kern_total = lax.psum(kern_local.astype(jnp.bfloat16), ("crop", "rows")).astype(jnp.float32)
    back_select = jnp.einsum(
        "tce,bcke->tckb", pre_grad, in_panel, preferred_element_type=jnp.float32
    )
    one_hot = (
        block_rows[:, :, None] == jnp.arange(block_count, dtype=jnp.int32)[None, None, :]
    ).astype(jnp.float32)
    token_terms = jnp.einsum(
        "tckb,ckr->trb", back_select, one_hot, precision=lax.Precision.HIGHEST
    ).reshape(crop_count, height, grid_width, depth_all)
    grad_tokens = lax.psum_scatter(
        token_terms.astype(jnp.bfloat16), "hid", scatter_dimension=3, tiled=True
    )
    first_term = jnp.einsum(
        "tckb,tce->bcke", in_select, pre_grad, preferred_element_type=jnp.float32
    )
    second_term = jnp.einsum(
        "tcf,tckd->fckd", mix_out, grad_select, preferred_element_type=jnp.float32
    )
    share_sums = lax.psum_scatter(
        (jnp.stack([first_term, second_term], axis=1) * loss_scale).astype(jnp.bfloat16),
        ("crop", "rows"),
        scatter_dimension=0,
        tiled=True,
    ).astype(jnp.float32)
    return (grad_tokens, share_sums[:, 0], share_sums[:, 1], kern_total)


def solution(mesh):
    placed = (
        P("crop", "rows", None, "hid"),
        P("crop", "rows", None, "hid"),
        P("rows", "hid", None, None),
        P("rows", "hid", None, None),
        P(None, "hid"),
        P("hid", None),
    )
    return jax.shard_map(
        on_device,
        mesh=mesh,
        in_specs=placed,
        out_specs=(
            P("crop", "rows", None, "hid"),
            P(("crop", "rows"), "hid", None, None),
            P(("crop", "rows"), "hid", None, None),
            P(None, "hid"),
        ),
        check_vma=False,
    )
```

profile of v0, /device:TPU:1, one launch (start us, length us, event | category | flops | bytes accessed | tf_op | source)
XLA Modules:
  0.0 376.9 jit_solution(11429003799002727429)
XLA Ops:
  13.2 34.1 %all-gather.9.cloned.1.call-done = bf16[1,2,64,4096]{3,2,1,0:T(8,128)(2,1)} async-done(((bf16[1,2,64,512]{3,2,1,0:T(8,128)(2,1)}), bf16[1,2,64,4096]{3,2,1,0:T(8,128)(2,1)}) %all-gather.9.cloned.1.call-update) | async-done | bytes 1048592 | tf_op jit(solution)/shard_map/all_gather | solution.py:40
  49.0 37.1 %all-gather.5.cloned.1.call-done = bf16[1,2,64,4096]{3,2,1,0:T(8,128)(2,1)} async-done(((bf16[1,2,64,512]{3,2,1,0:T(8,128)(2,1)}), bf16[1,2,64,4096]{3,2,1,0:T(8,128)(2,1)}) %all-gather.5.cloned.1.call-update) | async-done | bytes 1048592 | tf_op jit(solution)/shard_map/all_gather | solution.py:41
  87.9 2.4 gather_fusion.1
  90.3 2.4 gather_fusion
  92.7 4.6 %broadcast_select_fusion.1 = (bf16[40,128,256]{2,1,0:T(8,128)(2,1)S(1)}, bf16[40,128,256]{2,1,0:T(8,128)(2,1)}) fusion(bf16[40,128,256]{2,1,0:T(8,128)(2,1)} %gather_fusion, pred[40]{0:T(512)(128)(4,1)S(1)} %compare_and_fusion, bf16[40,128,256]{2,1,0:T(8,128)(2,1)} %gather_fusion.1), kind=kLoop, calls=%fused_computation.18 | loop fusion | flops 2621440 | bytes 10485800 | tf_op jit(solution)/shard_map/jit(_take)/select_n | solution.py:54
  97.3 36.7 %all-gather.7.cloned.1.call-done = bf16[256,8,5,256]{3,0,2,1:T(8,128)(2,1)} async-done(((bf16[16,8,5,256]{3,0,2,1:T(8,128)(2,1)}), bf16[256,8,5,256]{3,0,2,1:T(8,128)(2,1)}) %all-gather.7.cloned.1.call-update) | async-done | bytes 5242896 | tf_op jit(solution)/shard_map/all_gather | solution.py:37
  134.1 4.3 %fusion.9 = bf16[128,8,256]{2,0,1:T(8,128)(2,1)S(1)} fusion(bf16[128,8,5,256]{3,0,2,1:T(8,128)(2,1)S(1)} %bitcast.97, bf16[256,8,5,256]{3,0,2,1:T(8,128)(2,1)} %all-gather.7.cloned.1.call-done), kind=kOutput, calls=%fused_computation.39 | convolution fusion | flops 671350784 | bytes 8388608 | tf_op jit(solution)/shard_map/tckd,fckd->tcf/dot_general | solution.py:62
  140.8 2.8 collective-permute-start
  143.6 1.9 collective-permute-start.1
  146.9 7.7 %collective-permute-done.1 = bf16[1,1,64,2048]{3,2,1,0:T(8,128)(2,1)S(1)} collective-permute-done((bf16[1,1,64,2048]{3,2,1,0:T(8,128)(2,1)S(1)}, bf16[1,1,64,2048]{3,2,1,0:T(8,128)(2,1)S(1)}, u32[]{:S(2)}, u32[]{:S(2)}) %collective-permute-start.1) | collective-permute-done | bytes 262176 | tf_op jit(solution)/shard_map/ppermute | solution.py:19
  157.0 23.5 %all-gather.11.cloned.1.call-done = bf16[256,8,5,256]{3,0,2,1:T(8,128)(2,1)} async-done(((bf16[16,8,5,256]{3,0,2,1:T(8,128)(2,1)}), bf16[256,8,5,256]{3,0,2,1:T(8,128)(2,1)}) %all-gather.11.cloned.1.call-update) | async-done | bytes 5242896 | tf_op jit(solution)/shard_map/all_gather | solution.py:36
  180.6 5.1 %multiply_convert_fusion = (bf16[128,8,256]{2,0,1:T(8,128)(2,1)S(1)}, bf16[128,8,256]{2,0,1:T(8,128)(2,1)}) fusion(f32[128,8,256]{2,1,0:T(8,128)} %bitcast.108, bf16[128,8,5,256]{3,0,2,1:T(8,128)(2,1)S(1)} %bitcast.99, bf16[256,8,5,256]{3,0,2,1:T(8,128)(2,1)} %all-gather.11.cloned.1.call-done), kind=kOutput, calls=%fused_computation.76 | convolution fusion | flops 676593664 | bytes 9961472 | tf_op jit(solution)/shard_map/tckb,bcke->tce/dot_general | solution.py:57
  186.8 2.1 reshape.189
  190.0 2.7 collective-permute-start.2
  192.7 2.1 collective-permute-start.3
  194.8 2.7 convolution_bitcast_fusion.1
  197.5 2.9 collective-permute-done.3
  203.9 5.7 %fusion = bf16[256,2,8,5,256]{0,4,3,2,1:T(8,128)(2,1)} fusion(f32[256,1,8,5,256]{0,4,3,2,1:T(8,128)S(1)} %convolution_bitcast_fusion, f32[256,1,8,5,256]{0,4,3,2,1:T(8,128)S(1)} %convolution_bitcast_fusion.1), kind=kLoop, calls=%fused_computation.3 | loop fusion | flops 15728640 | bytes 31457280 | tf_op jit(solution)/shard_map/convert_element_type | solution.py:109
  209.6 15.4 %copy.56 = bf16[256,2,8,5,256]{4,2,3,1,0:T(8,128)(2,1)} copy(bf16[256,2,8,5,256]{0,4,3,2,1:T(8,128)(2,1)} %fusion) | data formatting | bytes 20971520 | tf_op jit(solution)/shard_map/convert_element_type | solution.py:109
  226.0 4.3 %convolution_bitcast_fusion.2 = f32[128,8,5,256]{3,0,2,1:T(8,128)S(1)} fusion(bf16[256,8,5,256]{3,0,2,1:T(8,128)(2,1)} %all-gather.11.cloned.1.call-done, bf16[128,8,256]{2,0,1:T(8,128)(2,1)S(1)} %copy-done.4), kind=kOutput, calls=%fused_computation.19 | convolution fusion | flops 671088640 | bytes 11010048 | tf_op jit(solution)/shard_map/tce,bcke->tckb/dot_general | solution.py:90
  230.3 5.9 %fusion.5 = bf16[128,16,256]{2,1,0:T(8,128)(2,1)} fusion(f32[128,8,5,256]{3,0,2,1:T(8,128)S(1)} %convolution_bitcast_fusion.2, s32[8,5]{0,1:T(8,128)S(1)} %copy.44), kind=kOutput, calls=%fused_computation.35 | convolution fusion | flops 252183168 | bytes 6291616 | tf_op jit(solution)/shard_map/tckb,ckr->trb/dot_general | solution.py:96
  236.2 2.3 convert_element_type.87
  239.8 119.7 %psum.7 = bf16[9,2048]{1,0:T(8,128)(2,1)S(1)} all-reduce(bf16[9,2048]{1,0:T(8,128)(2,1)S(1)} %multiply_convert_fusion.1), channel_id=1, replica_groups=mesh['crop'=2,'rows'=16,'hid'=8] {'crop','rows'}, use_global_device_ids=true, to_apply=%region_11.13 | all-reduce | flops 18432 | bytes 73728 | tf_op jit(solution)/shard_map/psum | solution.py:89
  362.0 8.0 %reduce-scatter.3.cloned.1.call-done = bf16[1,2,64,512]{3,2,1,0:T(8,128)(2,1)} async-done(((bf16[1,2,64,4096]{3,2,1,0:T(8,128)(2,1)}), bf16[1,2,64,512]{3,2,1,0:T(8,128)(2,1)}) %reduce-scatter.3.cloned.1.call-update) | async-done | bytes 131088 | tf_op jit(solution)/shard_map/reduce_scatter | solution.py:99
  (59 shorter events, 26.1 us)
Async XLA Ops:
  7.2 40.1 %all-gather.9.cloned.1.call-start = ((), (), s32[]{:S(2)}) async-start(), calls=%async_computation.4 | async-start | bytes 1179648 | tf_op jit(solution)/shard_map/all_gather | solution.py:40
  7.9 78.2 %all-gather.5.cloned.1.call-start = ((), (), s32[]{:S(2)}) async-start(), calls=%async_computation.2 | async-start | bytes 1179648 | tf_op jit(solution)/shard_map/all_gather | solution.py:41
  8.6 125.4 %all-gather.7.cloned.1.call-start = ((), (), s32[]{:S(2)}) async-start(), calls=%async_computation.3 | async-start | bytes 5570560 | tf_op jit(solution)/shard_map/all_gather | solution.py:37
  10.5 170.1 %all-gather.11.cloned.1.call-start = ((), (), s32[]{:S(2)}) async-start(), calls=%async_computation.5 | async-start | bytes 5570560 | tf_op jit(solution)/shard_map/all_gather | solution.py:36
  12.3 347.8 %reduce-scatter.5.cloned.1.call-start = ((), (), s32[]{:S(2)}) async-start(), calls=%async_computation.7 | async-start | bytes 10813440 | tf_op jit(solution)/shard_map/reduce_scatter | solution.py:108
  97.3 41.1 %copy-start = (bf16[40,128,256]{2,1,0:T(8,128)(2,1)}, bf16[40,128,256]{2,1,0:T(8,128)(2,1)S(1)}, u32[]{:S(2)}) copy-start(bf16[40,128,256]{2,1,0:T(8,128)(2,1)S(1)} %get-tuple-element.43) | copy-start | bytes 7864324
  138.4 7.1 %copy-start.5 = (f32[9,2048]{1,0:T(8,128)S(1)}, f32[9,2048]{1,0:T(8,128)}, u32[]{:S(2)}) copy-start(f32[9,2048]{1,0:T(8,128)} %param.12) | copy-start | bytes 221188
  140.8 6.1 %collective-permute-start = (bf16[1,1,64,2048]{3,2,1,0:T(8,128)(2,1)S(1)}, bf16[1,1,64,2048]{3,2,1,0:T(8,128)(2,1)S(1)}, u32[]{:S(2)}, u32[]{:S(2)}) collective-permute-start(bf16[1,1,64,2048]{3,2,1,0:T(8,128)(2,1)S(1)} %get-tuple-element.32), channel_id=1, source_target_pairs={{0,8},{8,16},{16,24},{24,32},{32,40},{40,48},{48,56},{56,64},{64,7... | collective-permute-start | bytes 786440 | tf_op jit(solution)/shard_map/ppermute | solution.py:18
  143.6 11.0 %collective-permute-start.1 = (bf16[1,1,64,2048]{3,2,1,0:T(8,128)(2,1)S(1)}, bf16[1,1,64,2048]{3,2,1,0:T(8,128)(2,1)S(1)}, u32[]{:S(2)}, u32[]{:S(2)}) collective-permute-start(bf16[1,1,64,2048]{3,2,1,0:T(8,128)(2,1)S(1)} %get-tuple-element.33), channel_id=1, source_target_pairs={{8,0},{16,8},{24,16},{32,24},{40,32},{48,40},{56,48},{64,56},{72,6... | collective-permute-start | bytes 786440 | tf_op jit(solution)/shard_map/ppermute | solution.py:19
  154.8 25.8 %copy-start.2 = (bf16[40,128,256]{2,1,0:T(8,128)(2,1)S(1)}, bf16[40,128,256]{2,1,0:T(8,128)(2,1)}, u32[]{:S(2)}) copy-start(bf16[40,128,256]{2,1,0:T(8,128)(2,1)} %get-tuple-element.44) | copy-start | bytes 7864324
  190.0 7.5 %collective-permute-start.2 = (bf16[1,1,64,2048]{3,2,1,0:T(8,128)(2,1)S(1)}, bf16[1,1,64,2048]{3,2,1,0:T(8,128)(2,1)S(1)}, u32[]{:S(2)}, u32[]{:S(2)}) collective-permute-start(bf16[1,1,64,2048]{3,2,1,0:T(8,128)(2,1)S(1)} %get-tuple-element.30), channel_id=1, source_target_pairs={{0,8},{8,16},{16,24},{24,32},{32,40},{40,48},{48,56},{56,64},{64,7... | collective-permute-start | bytes 786440 | tf_op jit(solution)/shard_map/ppermute | solution.py:18
  192.7 7.7 %collective-permute-start.3 = (bf16[1,1,64,2048]{3,2,1,0:T(8,128)(2,1)S(1)}, bf16[1,1,64,2048]{3,2,1,0:T(8,128)(2,1)S(1)}, u32[]{:S(2)}, u32[]{:S(2)}) collective-permute-start(bf16[1,1,64,2048]{3,2,1,0:T(8,128)(2,1)S(1)} %get-tuple-element.31), channel_id=1, source_target_pairs={{8,0},{16,8},{24,16},{32,24},{40,32},{48,40},{56,48},{64,56},{72,6... | collective-permute-start | bytes 786440 | tf_op jit(solution)/shard_map/ppermute | solution.py:19
  194.8 5.6 %copy-start.3 = (bf16[1,2,64,2048]{3,2,1,0:T(8,128)(2,1)S(1)}, bf16[1,2,64,2048]{3,2,1,0:T(8,128)(2,1)}, u32[]{:S(2)}) copy-start(bf16[1,2,64,2048]{3,2,1,0:T(8,128)(2,1)} %reshape.189) | copy-start | bytes 1572868
  200.5 1.7 copy-start.1
  225.0 0.7 copy-start.6
  225.0 1.1 copy-start.4
  225.0 145.0 %reduce-scatter.3.cloned.1.call-start = ((), (), s32[]{:S(2)}) async-start(), calls=%async_computation.6 | async-start | bytes 1179648 | tf_op jit(solution)/shard_map/reduce_scatter | solution.py:99
Sparse Core Ops, SparseCore 0:
  9.8 37.3 all-gather.8
  49.0 37.0 all-gather.4
  88.5 45.5 all-gather.6
  136.3 44.2 all-gather.10
  225.1 107.0 reduce-scatter.4
  335.3 34.6 reduce-scatter.2
where the time goes:
time: 381 us; the launch traced here: 377 us
  waiting for transfers between devices  153 us (40%)
  blocking collectives  120 us (31%)
  local copies, waits for them, and re-layouts  41.1 us (11%)
  matrix products  23.8 us (6%)
  other arithmetic  15.2 us (4%)
  between operations  14.3 us (4%)
  starting transfers between devices  9.96 us (3%)
    psum x1, blocking collectives, on_device(): lax.psum(kern_local.astype(jnp.bfloat16), ('crop', 'rows'))  120 us
    all_gather x1, waiting for transfers between devices, on_device(): lax.all_gather(cotangent, 'hid', axis=3, tiled=True)  37.1 us
    all_gather x1, waiting for transfers between devices, on_device(): lax.all_gather(weight_out, 'rows', axis=0, tiled=True)  36.7 us
    all_gather x1, waiting for transfers between devices, on_device(): lax.all_gather(tokens, 'hid', axis=3, tiled=True)  34.1 us
    all_gather x1, waiting for transfers between devices, on_device(): lax.all_gather(weight_in, 'rows', axis=0, tiled=True)  23.5 us
    convert_element_type x1, local copies, waits for them, and re-layouts, on_device(): (jnp.stack([first_term, second_term], axis=1) * loss_scale).astype(jnp.bf...  15.4 us
    ppermute x2, waiting for transfers between devices, padded(): after = lax.ppermute(initial, axis, down)  10.6 us
    unnamed x21, local copies, waits for them, and re-layouts  9.42 us
  transfers between devices with their start and end apart: 10, of which 8 were waited for; matrix products, arithmetic and copies ran while one was open for 12% of the time, Pallas kernels for 0%

commit v1 on v0

v1 whole, which is shorter than its diff:
```python
import functools

import jax
import jax.numpy as jnp
from jax import lax
from jax.experimental import pallas as pl
from jax.experimental.pallas import tpu as pltpu
from jax.sharding import PartitionSpec as P

root_two_pi = 0.7978845608
cubic_coef = 0.044715
loss_scale = 0.03125

F32, BF16 = jnp.float32, jnp.bfloat16
NX, NY, NC = 4, 4, 2
COLS, NNZ, BS, PW = 4, 5, 256, 64
TOK = 256
CORE, XPOS, YPOS, YLO = 20, 21, 22, 23
ANY = pl.BlockSpec(memory_space=pl.ANY)


def row_perm(move):
    pairs = []
    for y in range(2):
        for x in range(NX):
            for c in range(NC):
                y2, x2, c2 = move(y, x, c)
                pairs.append(((y * NX + x) * NC + c, (y2 * NX + x2 % NX) * NC + c2))
    return pairs


def along_x(value, step):
    return lax.ppermute(value, "rows", row_perm(lambda y, x, c: (y, x + step, c)))


def to_partner(value):
    return lax.ppermute(value, "rows", row_perm(lambda y, x, c: (y, x, 1 - c)))


def along_y(value, step):
    pairs = [(y * 8 + r, (y + step) % NY * 8 + r) for y in range(NY) for r in range(8)]
    return lax.ppermute(value, ("crop", "rows"), pairs)


def to_next_chip(value, step):
    pairs = []
    for q in range(8):
        if 0 <= q + step < 8:
            pairs += [(q * 2 + c, (q + step) * 2 + c) for c in range(NC)]
    return lax.ppermute(value, "rows", pairs)


def dot(a, b, dims):
    return lax.dot_general(a, b, (dims, ((), ())), preferred_element_type=F32)


def params():
    return pltpu.CompilerParams(dimension_semantics=("arbitrary",), vmem_limit_bytes=48 * 2**20)


def start_tokens(meta, own, other, which, buf, sem):
    core = meta[CORE]
    for src, at in ((own, core), (other, 1 - core)):
        rows = pl.ds(pl.multiple_of(at * 128, 128), 128)
        for half in range(2):
            pltpu.make_async_copy(
                src.at[:, which, :, pl.ds(half * BS, BS)], buf.at[:, half, rows], sem
            ).start()


def wait_all(buf, sem):
    pltpu.make_async_copy(buf, buf, sem).wait()


def start_weights(meta, pieces, which, buf, sems):
    x, ylo = meta[XPOS], meta[YLO]
    own, xm, xp, x2, yo, ym, yp, y2a, y2b = pieces
    here, there = ylo * NX, (1 - ylo) * NX
    at = lambda base, d: base + (x + d) % NX
    plan = []
    for s in range(2):
        plan += [
            (own, s, at(here, 0), s),
            (xm, s, at(here, 3), s),
            (xp, s, at(here, 1), s),
            (x2, s, at(here, 2), s),
            (yo, s, at(there, 0), s),
            (ym, s, at(there, 3), s),
            (yp, s, at(there, 1), s),
        ]
    plan += [(y2a, 0, at(there, 2), 0), (y2b, 0, at(there, 2), 1)]
    for c in range(COLS):
        for src, row, j, s in plan:
            pltpu.make_async_copy(src.at[row, which, c], buf.at[c, :, 2 * j + s], sems.at[c]).start()


def token_block(buf, row):
    return buf[row // 2, row % 2]


def forward_kernel(which, meta, own, other, *refs):
    pieces, refs = refs[:9], refs[9:]
    if which == 0:
        pre_ref, act_ref, top_ref, bot_ref, tok, wts, tok_sem, w_sems = refs
    else:
        act_ref, top_ref, bot_ref, tok, wts, tok_sem, w_sems = refs
    c = pl.program_id(0)

    @pl.when(c == 0)
    def _():
        start_tokens(meta, own, other, which, tok, tok_sem)
        start_weights(meta, pieces, which, wts, w_sems)
        wait_all(tok, tok_sem)

    wait_all(wts.at[c], w_sems.at[c])
    dims = ((1,), (0,)) if which == 0 else ((1,), (1,))
    total = jnp.zeros((TOK, BS), F32)
    for k in range(NNZ):
        total += dot(token_block(tok, meta[c * NNZ + k]), wts[c, k].reshape(BS, BS), dims)
    if which == 0:
        pre_ref[...] = total
        inner = root_two_pi * (total + cubic_coef * total * total * total)
        total = 0.5 * total * (1.0 + jnp.tanh(inner))
    out = total.astype(BF16)
    act_ref[...] = out
    top_ref[...] = out[:PW]
    bot_ref[...] = out[TOK - PW :]


def column(rows):
    return pl.BlockSpec((rows, BS), lambda c, m: (0, c))


def forward(which, meta, own, other, pieces):
    outs = [(TOK, BF16), (PW, BF16), (PW, BF16)]
    if which == 0:
        outs = [(TOK, F32)] + outs
    return pl.pallas_call(
        functools.partial(forward_kernel, which),
        out_shape=[jax.ShapeDtypeStruct((r, COLS * BS), t) for r, t in outs],
        grid_spec=pltpu.PrefetchScalarGridSpec(
            num_scalar_prefetch=1,
            grid=(COLS,),
            in_specs=[ANY] * 11,
            out_specs=[column(r) for r, _ in outs],
            scratch_shapes=[
                pltpu.VMEM((8, 2, TOK, BS), BF16),
                pltpu.VMEM((COLS, NNZ, 16, 16, BS), BF16),
                pltpu.SemaphoreType.DMA,
                pltpu.SemaphoreType.DMA((COLS,)),
            ],
        ),
        compiler_params=params(),
        cost_estimate=pl.CostEstimate(
            flops=2 * TOK * BS * BS * NNZ * COLS, transcendentals=TOK * BS * COLS, bytes_accessed=7 * 2**20
        ),
        name=("preact", "mixgrad")[which],
    )(meta, own, other, *pieces)


def shifted_rows(mid, up, down):
    cells = lax.broadcasted_iota(jnp.int32, (PW, BS), 0)
    out = []
    for row in [up[...]] + [mid[i * PW : (i + 1) * PW] for i in range(4)] + [down[...]]:
        row = row.astype(F32)
        left = jnp.where(cells == 0, 0.0, pltpu.roll(row, 1, 0))
        right = jnp.where(cells == PW - 1, 0.0, pltpu.roll(row, PW - 1, 0))
        out.append((left, row, right))
    return out


def grad_out_kernel(meta, own, other, act, up, down, mgrad, taps, *refs):
    outs, (cot, mixed, res, sem) = refs[:NX], refs[NX:]
    c = pl.program_id(0)
    x = meta[XPOS]

    @pl.when(c == 0)
    def _():
        start_tokens(meta, own, other, 1, cot, sem)

    rows = shifted_rows(act, up, down)
    for i in range(4):
        total = jnp.zeros((PW, BS), F32)
        for a in range(3):
            for b in range(3):
                total += taps[3 * a + b : 3 * a + b + 1] * rows[i + a][b]
        mixed[i * PW : (i + 1) * PW] = total.astype(BF16)
    sums = []
    for a in range(3):
        for b in range(3):
            total = jnp.zeros((PW, BS), F32)
            for i in range(4):
                total += rows[i + a][b] * mgrad[i * PW : (i + 1) * PW].astype(F32)
            sums.append(jnp.sum(total, axis=0, keepdims=True))
    slab = jnp.concatenate(sums + [jnp.zeros((7, BS), F32)], axis=0) * loss_scale
    for d in range(NX):
        outs[d][0, 20] = slab.astype(BF16)

    @pl.when(c == 0)
    def _():
        wait_all(cot, sem)

    mix = mixed[...]
    for k in range(NNZ):
        part = dot(mix, token_block(cot, meta[c * NNZ + k]), ((0,), (0,))) * loss_scale
        res[k] = part.astype(BF16).reshape(16, 16, BS)
        for d in range(NX):
            for y in range(NY):
                outs[d][0, k * NY + y] = res[k, y * NX + (x + d) % NX]


def slabs(count):
    return pl.BlockSpec((1, count, 16, BS), lambda c, m: (c, 0, 0, 0))


def taps_spec():
    return pl.BlockSpec((9, BS), lambda c, m: (0, m[CORE] * COLS + c))


def grad_out(meta, own, other, act, up, down, mgrad, taps):
    return pl.pallas_call(
        grad_out_kernel,
        out_shape=[jax.ShapeDtypeStruct((COLS, 21, 16, BS), BF16)] * NX,
        grid_spec=pltpu.PrefetchScalarGridSpec(
            num_scalar_prefetch=1,
            grid=(COLS,),
            in_specs=[ANY, ANY, column(TOK), column(PW), column(PW), column(TOK), taps_spec()],
            out_specs=[slabs(21)] * NX,
            scratch_shapes=[
                pltpu.VMEM((8, 2, TOK, BS), BF16),
                pltpu.VMEM((TOK, BS), BF16),
                pltpu.VMEM((NNZ, 16, 16, BS), BF16),
                pltpu.SemaphoreType.DMA,
            ],
        ),
        compiler_params=params(),
        cost_estimate=pl.CostEstimate(
            flops=2 * TOK * BS * BS * NNZ * COLS, transcendentals=0, bytes_accessed=7 * 2**20
        ),
        name="gradout",
    )(meta, own, other, act, up, down, mgrad, taps)


def grad_in_kernel(meta, own, other, *refs):
    pieces, refs = refs[:9], refs[9:]
    pre, mgrad, up, down, taps = refs[:5]
    outs, (keep, send, tok, wts, pgrad, res, acc, sem, w_sems) = refs[5 : 5 + NY], refs[5 + NY :]
    c = pl.program_id(0)
    core, y_here = meta[CORE], meta[YPOS]

    @pl.when(c == 0)
    def _():
        start_tokens(meta, own, other, 0, tok, sem)
        start_weights(meta, pieces, 0, wts, w_sems)
        acc[...] = jnp.zeros_like(acc)

    rows = shifted_rows(mgrad, up, down)
    for i in range(4):
        part = pl.ds(i * PW, PW)
        total = jnp.zeros((PW, BS), F32)
        for a in range(3):
            for b in range(3):
                total += taps[3 * a + b : 3 * a + b + 1] * rows[i + 2 - a][2 - b]
        p = pre[part]
        t = jnp.tanh(root_two_pi * (p + cubic_coef * p * p * p))
        slope = 0.5 * (1.0 + t) + 0.5 * p * (1.0 - t * t) * root_two_pi * (1.0 + 3.0 * cubic_coef * p * p)
        pgrad[part] = (total * slope).astype(BF16)

    @pl.when(c == 0)
    def _():
        wait_all(tok, sem)

    wait_all(wts.at[c], w_sems.at[c])
    grads = pgrad[...]
    for k in range(NNZ):
        row = meta[c * NNZ + k]
        acc[row] += dot(grads, wts[c, k].reshape(BS, BS), ((1,), (1,)))
        part = dot(token_block(tok, row), grads, ((0,), (0,))) * loss_scale
        res[k] = part.astype(BF16).reshape(16, 16, BS)
        for d in range(NY):
            for x in range(NX):
                outs[d][0, k * NX + x] = res[k, (y_here + d) % NY * NX + x]

    @pl.when(c == COLS - 1)
    def _():
        keep[...] = acc[:, pl.ds(pl.multiple_of(core * 128, 128), 128)].astype(BF16)
        send[...] = acc[:, pl.ds(pl.multiple_of((1 - core) * 128, 128), 128)].astype(BF16)


def grad_in(meta, own, other, pieces, pre, mgrad, up, down, taps):
    half = pl.BlockSpec((16, 128, BS), lambda c, m: (0, 0, 0))
    return pl.pallas_call(
        grad_in_kernel,
        out_shape=[jax.ShapeDtypeStruct((COLS, 20, 16, BS), BF16)] * NY
        + [jax.ShapeDtypeStruct((16, 128, BS), BF16)] * 2,
        grid_spec=pltpu.PrefetchScalarGridSpec(
            num_scalar_prefetch=1,
            grid=(COLS,),
            in_specs=[ANY] * 11 + [column(TOK), column(TOK), column(PW), column(PW), taps_spec()],
            out_specs=[slabs(20)] * NY + [half, half],
            scratch_shapes=[
                pltpu.VMEM((8, 2, TOK, BS), BF16),
                pltpu.VMEM((COLS, NNZ, 16, 16, BS), BF16),
                pltpu.VMEM((TOK, BS), BF16),
                pltpu.VMEM((NNZ, 16, 16, BS), BF16),
                pltpu.VMEM((16, TOK, BS), F32),
                pltpu.SemaphoreType.DMA,
                pltpu.SemaphoreType.DMA((COLS,)),
            ],
        ),
        compiler_params=params(),
        cost_estimate=pl.CostEstimate(
            flops=4 * TOK * BS * BS * NNZ * COLS, transcendentals=TOK * BS * COLS, bytes_accessed=12 * 2**20
        ),
        name="gradin",
    )(meta, own, other, *pieces, pre, mgrad, up, down, taps)


def first_sum_kernel(pos, extra, meta, a, b, e, f, *outs):
    here = meta[pos]
    for d in range(4):
        for k in range(NNZ):
            at = k * 4 + (here + d) % 4
            total = a[0, at].astype(F32) + b[0, at].astype(F32) + e[0, at].astype(F32) + f[0, at].astype(F32)
            outs[d][0, k] = total.astype(BF16)
        if extra:
            total = a[0, 20].astype(F32) + b[0, 20].astype(F32) + e[0, 20].astype(F32) + f[0, 20].astype(F32)
            outs[d][0, NNZ] = total.astype(BF16)


def first_sum(pos, extra, meta, parts):
    count = NNZ + extra
    return pl.pallas_call(
        functools.partial(first_sum_kernel, pos, extra),
        out_shape=[jax.ShapeDtypeStruct((COLS, count, 16, BS), BF16)] * 4,
        grid_spec=pltpu.PrefetchScalarGridSpec(
            num_scalar_prefetch=1,
            grid=(COLS,),
            in_specs=[slabs(20 + extra)] * 4,
            out_specs=[slabs(count)] * 4,
        ),
        compiler_params=params(),
        cost_estimate=pl.CostEstimate(flops=2**21, transcendentals=0, bytes_accessed=7 * 2**19),
        name="firstsum",
    )(meta, *parts)


def second_sum_kernel(meta, *refs):
    a_parts, b_parts, (keep, send) = refs[:4], refs[4:8], refs[8:]
    core = meta[CORE]

    def total(parts, c, k):
        return sum(p[c, k].astype(F32) for p in parts)

    for c in range(COLS):
        for w, parts in ((0, b_parts), (1, a_parts)):
            for k in range(NNZ):
                val = total(parts, c, k)
                low, high = val[:8], val[8:]
                keep[w, c, k] = jnp.where(core == 0, low, high)
                send[w, c, k] = jnp.where(core == 0, high, low).astype(BF16)
        slab = total(a_parts, c, NNZ)
        for part in range(2):
            half = slab[part * 8 : part * 8 + 8]
            keep[part, c, NNZ] = half.astype(BF16).astype(F32)
            send[part, c, NNZ] = half.astype(BF16)


def second_sum(meta, a_parts, b_parts):
    shape = (2, COLS, NNZ + 1, 8, BS)
    vmem = pl.BlockSpec(memory_space=pltpu.VMEM)
    return pl.pallas_call(
        second_sum_kernel,
        out_shape=[jax.ShapeDtypeStruct(shape, F32), jax.ShapeDtypeStruct(shape, BF16)],
        in_specs=[pl.BlockSpec(memory_space=pltpu.SMEM)] + [vmem] * 8,
        out_specs=[vmem] * 2,
        compiler_params=pltpu.CompilerParams(vmem_limit_bytes=48 * 2**20),
        name="secondsum",
    )(meta, *a_parts, *b_parts)


def place_kernel(meta, keep, got, win, wout, kern):
    first = meta[CORE] == 0
    for w, out in ((0, win), (1, wout)):
        for k in range(NNZ):
            mine = [keep[w, c, k] for c in range(COLS)]
            its = [got[w, c, k].astype(F32) for c in range(COLS)]
            low = [jnp.where(first, m, i) for m, i in zip(mine, its)]
            high = [jnp.where(first, i, m) for m, i in zip(mine, its)]
            block = jnp.stack(low + high, axis=0)
            out[:, k] = jnp.swapaxes(block, 0, 1)
    for c in range(COLS):
        mine = jnp.concatenate([keep[0, c, NNZ], keep[1, c, NNZ]], axis=0)[:9]
        its = jnp.concatenate([got[0, c, NNZ].astype(F32), got[1, c, NNZ].astype(F32)], axis=0)[:9]
        kern[:, c * BS : (c + 1) * BS] = jnp.where(first, mine, its)
        kern[:, (COLS + c) * BS : (COLS + c + 1) * BS] = jnp.where(first, its, mine)


def place(meta, keep, got):
    vmem = pl.BlockSpec(memory_space=pltpu.VMEM)
    return pl.pallas_call(
        place_kernel,
        out_shape=[
            jax.ShapeDtypeStruct((8, NNZ, 8, BS), F32),
            jax.ShapeDtypeStruct((8, NNZ, 8, BS), F32),
            jax.ShapeDtypeStruct((9, 8 * BS), F32),
        ],
        in_specs=[pl.BlockSpec(memory_space=pltpu.SMEM), vmem, vmem],
        out_specs=[vmem] * 3,
        compiler_params=pltpu.CompilerParams(vmem_limit_bytes=48 * 2**20),
        name="place",
    )(meta, keep, got)


def on_device(tokens, cotangent, weight_in, weight_out, mix_kernel, block_rows):
    row, crop = lax.axis_index("rows"), lax.axis_index("crop")
    core, x, ylo = row % 2, row // 2 % NX, row // 8
    my_rows = lax.dynamic_slice_in_dim(block_rows, core * COLS, COLS, axis=0).reshape(-1)
    meta = jnp.concatenate([my_rows, jnp.stack([core, x, crop * 2 + ylo, ylo]).astype(jnp.int32)])

    both = jnp.stack([tokens.reshape(128, 512), cotangent.reshape(128, 512)])
    own = lax.all_gather(both, "hid", axis=0)

    panels = jnp.stack([weight_in, weight_out]).reshape(2, 16, 2, COLS, NNZ, BS)
    panels = panels.transpose(2, 0, 3, 4, 1, 5)
    mine = lax.dynamic_index_in_dim(panels, core, 0, keepdims=False)
    theirs = lax.dynamic_index_in_dim(panels, 1 - core, 0, keepdims=False)
    got = to_partner(theirs)
    piece = jnp.stack([jnp.where(core == 0, mine, got), jnp.where(core == 0, got, mine)])
    xm, xp = along_x(piece, 1), along_x(piece, -1)
    yo = along_y(piece, 1)
    x2 = along_x(piece, 2)
    ym, yp = along_y(xm, 1), along_y(xp, -1)
    y2a, y2b = along_y(x2[:1], 1), along_y(x2[1:], -1)
    pieces = (piece, xm, xp, x2, yo, ym, yp, y2a, y2b)

    other = to_partner(own)
    pre, act, act_top, act_bot = forward(0, meta, own, other, pieces)
    act_up, act_down = to_next_chip(act_bot, 1), to_next_chip(act_top, -1)
    mgrad, mg_top, mg_bot = forward(1, meta, own, other, pieces)
    mg_up, mg_down = to_next_chip(mg_bot, 1), to_next_chip(mg_top, -1)

    outs = grad_out(meta, own, other, act, act_up, act_down, mgrad, mix_kernel)
    a_parts = (outs[0], along_x(outs[1], 1), along_x(outs[3], -1), along_x(outs[2], 2))
    *ins, keep, send = grad_in(meta, own, other, pieces, pre, mgrad, mg_up, mg_down, mix_kernel)
    b_parts = (ins[0], along_y(ins[1], 1), along_y(ins[3], -1), along_y(ins[2], 2))

    terms = (keep.astype(F32) + to_partner(send).astype(F32)).astype(BF16)
    shares = lax.psum_scatter(terms.reshape(8, 2, 128, BS), "hid", scatter_dimension=0, tiled=True)
    grad_tokens = shares.reshape(2, 128, BS).transpose(1, 0, 2).reshape(1, 2, PW, 512)

    a_next = first_sum(YPOS, 1, meta, a_parts)
    a_last = (a_next[0], along_y(a_next[1], 1), along_y(a_next[3], -1), along_y(a_next[2], 2))
    b_next = first_sum(XPOS, 0, meta, b_parts)
    b_last = (b_next[0], along_x(b_next[1], 1), along_x(b_next[3], -1), along_x(b_next[2], 2))
    kept, sent = second_sum(meta, a_last, b_last)
    win, wout, kern = place(meta, kept, to_partner(sent))
    return grad_tokens, win.transpose(0, 2, 1, 3), wout.transpose(0, 2, 1, 3), kern


def solution(mesh):
    placed = (
        P("crop", "rows", None, "hid"),
        P("crop", "rows", None, "hid"),
        P("rows", "hid", None, None),
        P("rows", "hid", None, None),
        P(None, "hid"),
        P("hid", None),
    )
    return jax.shard_map(
        on_device,
        mesh=mesh,
        in_specs=placed,
        out_specs=(
            P("crop", "rows", None, "hid"),
            P(("crop", "rows"), "hid", None, None),
            P(("crop", "rows"), "hid", None, None),
            P(None, "hid"),
        ),
        check_vma=False,
    )
```

time: 381 us -> 228 us (0.60)
  blocking collectives: 120 us -> 0 us
  starting transfers between devices: 9.96 us -> 64 us
  waiting for transfers between devices: 153 us -> 112 us
  local copies, waits for them, and re-layouts: 41.1 us -> 5.9 us
  Pallas kernels: 0 us -> 26.8 us
  matrix products: 23.8 us -> 0 us
  other arithmetic: 15.2 us -> 4.49 us
    psum x1 -> x0, blocking collectives: 120 us -> none  [on_device(): lax.psum(kern_local.astype(jnp.bfloat16), ('crop', 'rows'))]
    all_gather x4 -> x1, waiting for transfers between devices: 131 us -> 40.5 us  [on_device(): own = lax.all_gather(both, 'hid', axis=0)]
    ppermute x4 -> x28, waiting for transfers between devices: 11.9 us -> 71 us  [the longest x9 44 us: along_x(): lax.ppermute(value, 'rows', row_perm(lambda y, x, c: (y, x + step, c)))]
    ppermute x4 -> x28, starting transfers between devices: 9.5 us -> 63.9 us  [the longest x9 24 us: along_x(): lax.ppermute(value, 'rows', row_perm(lambda y, x, c: (y, x + step, c)))]
    pallas_call x0 -> x8, Pallas kernels: none -> 26.8 us  [the longest x2 8.63 us: forward(): pl.pallas_call(functools.partial(forward_kernel, which), out_shape=[jax.S...]
    dot_general x6 -> x0, matrix products: 23.8 us -> none  [the longest x1 5.85 us: on_device(): jnp.einsum('tckb,ckr->trb', back_select, one_hot, precision=lax.Precision...]
    convert_element_type x4 -> x0, local copies, waits for them, and re-layouts: 19.9 us -> none  [the longest x1 15.4 us: on_device(): (jnp.stack([first_term, second_term], axis=1) * loss_scale).astype(jnp.bf...]
    reduce_scatter x2 -> x1, waiting for transfers between devices: 8.02 us -> 0.01 us  [on_device(): lax.psum_scatter(terms.reshape(8, 2, 128, BS), 'hid', scatter_dimension=0...]
  transfers between devices with their start and end apart: 10 -> 30, of which waited for: 8 -> 12; matrix products, arithmetic and copies ran while one was open for 12% -> 2% of each run, Pallas kernels for 0% -> 6%
where the time goes in v1:
time: 228 us; the launch traced here: 227 us
  waiting for transfers between devices  112 us (49%)
  starting transfers between devices  64 us (28%)
  Pallas kernels  26.8 us (12%)
  between operations  14.4 us (6%)
  local copies, waits for them, and re-layouts  5.9 us (3%)
  other arithmetic  4.49 us (2%)
    ppermute x9, waiting for transfers between devices, along_x(): lax.ppermute(value, 'rows', row_perm(lambda y, x, c: (y, x + step, c)))  44 us
    all_gather x1, waiting for transfers between devices, on_device(): own = lax.all_gather(both, 'hid', axis=0)  40.5 us
    ppermute x9, starting transfers between devices, along_x(): lax.ppermute(value, 'rows', row_perm(lambda y, x, c: (y, x + step, c)))  24 us
    ppermute x11, starting transfers between devices, along_y(): return lax.ppermute(value, ('crop', 'rows'), pairs)  22.3 us
    ppermute x11, waiting for transfers between devices, along_y(): return lax.ppermute(value, ('crop', 'rows'), pairs)  19.5 us
    ppermute x4, starting transfers between devices, to_partner(): return lax.ppermute(value, 'rows', row_perm(lambda y, x, c: (y, x, 1 - c)))  12.3 us
    pallas_call x2, Pallas kernels, forward(): pl.pallas_call(functools.partial(forward_kernel, which), out_shape=[jax.S...  8.63 us
    pallas_call x1, Pallas kernels, grad_in(): pl.pallas_call(grad_in_kernel, out_shape=[jax.ShapeDtypeStruct((COLS, 20,...  8.62 us
  transfers between devices with their start and end apart: 30, of which 12 were waited for; matrix products, arithmetic and copies ran while one was open for 2% of the time, Pallas kernels for 6%

profile of v1, /device:TPU:1, one launch (start us, length us, event | category | flops | bytes accessed | tf_op | source)
XLA Modules:
  0.0 227.2 jit_solution(17239447428675221653)
XLA Ops:
  11.1 40.5 %all-gather.3.cloned.1.call-done = bf16[16,128,512]{2,1,0:T(8,128)(2,1)} async-done(((bf16[2,128,512]{2,1,0:T(8,128)(2,1)}), bf16[16,128,512]{2,1,0:T(8,128)(2,1)}) %all-gather.3.cloned.1.call-update) | async-done | bytes 2097168 | tf_op jit(solution)/shard_map/all_gather | solution.py:422
  51.6 4.4 %collective-permute-start = (bf16[8,2,128,512]{3,2,1,0:T(8,128)(2,1)}, bf16[8,2,128,512]{3,2,1,0:T(8,128)(2,1)}, u32[]{:S(2)}, u32[]{:S(2)}) collective-permute-start(bf16[8,2,128,512]{3,2,1,0:T(8,128)(2,1)} %bitcast.31), channel_id=1, source_target_pairs={{0,8},{8,0},{16,24},{24,16},{32,40},{40,32},{48,56},{56,48},{64,72... | collective-permute-start | bytes 6291464 | tf_op jit(solution)/shard_map/ppermute | solution.py:37
  56.2 4.0 %collective-permute-done.1 = bf16[2,4,5,16,256]{4,3,2,1,0:T(8,128)(2,1)S(1)} collective-permute-done((bf16[2,4,5,16,256]{4,3,2,1,0:T(8,128)(2,1)S(1)}, bf16[2,4,5,16,256]{4,3,2,1,0:T(8,128)(2,1)S(1)}, u32[]{:S(2)}, u32[]{:S(2)}) %collective-permute-start.1) | collective-permute-done | bytes 327712 | tf_op jit(solution)/shard_map/ppermute | solution.py:37
  60.3 2.5 %collective-permute-start.3 = (bf16[2,2,4,5,16,256]{5,4,3,2,1,0:T(8,128)(2,1)S(1)}, bf16[2,2,4,5,16,256]{5,4,3,2,1,0:T(8,128)(2,1)S(1)}, u32[]{:S(2)}, u32[]{:S(2)}) collective-permute-start(bf16[2,2,4,5,16,256]{5,4,3,2,1,0:T(8,128)(2,1)S(1)} %pad_maximum_fusion.refs_0_), channel_id=1, source_target_pairs={{0,48},{8,56},{16,0},{24,8},{32,16},{40,24},{48,32},{56,40},{64,11... | collective-permute-start | bytes 1966088 | tf_op jit(solution)/shard_map/ppermute | solution.py:33
  65.7 24.9 %collective-permute-done.3.refs_2_ = bf16[2,2,4,5,16,256]{5,4,3,2,1,0:T(8,128)(2,1)S(1)} collective-permute-done((bf16[2,2,4,5,16,256]{5,4,3,2,1,0:T(8,128)(2,1)S(1)}, bf16[2,2,4,5,16,256]{5,4,3,2,1,0:T(8,128)(2,1)S(1)}, u32[]{:S(2)}, u32[]{:S(2)}) %collective-permute-start.3) | collective-permute-done | bytes 655392 | tf_op jit(solution)/shard_map/ppermute | solution.py:33
  94.1 2.7 %collective-permute-start.9 = (bf16[1,2,4,5,16,256]{5,4,3,2,1,0:T(8,128)(2,1)}, bf16[1,2,4,5,16,256]{5,4,3,2,1,0:T(8,128)(2,1)}, u32[]{:S(2)}, u32[]{:S(2)}) collective-permute-start(bf16[1,2,4,5,16,256]{5,4,3,2,1,0:T(8,128)(2,1)} %get-tuple-element.66), channel_id=1, source_target_pairs={{0,192},{8,200},{16,208},{24,216},{32,224},{40,232},{48,240},{56,2... | collective-permute-start | bytes 983048 | tf_op jit(solution)/shard_map/ppermute | solution.py:42
  97.1 16.1 %collective-permute-done.9.refs_8_ = bf16[1,2,4,5,16,256]{5,4,3,2,1,0:T(8,128)(2,1)} collective-permute-done((bf16[1,2,4,5,16,256]{5,4,3,2,1,0:T(8,128)(2,1)}, bf16[1,2,4,5,16,256]{5,4,3,2,1,0:T(8,128)(2,1)}, u32[]{:S(2)}, u32[]{:S(2)}) %collective-permute-start.9) | collective-permute-done | bytes 327712 | tf_op jit(solution)/shard_map/ppermute | solution.py:42
  113.1 2.5 %collective-permute-done.8.refs_7_ = bf16[1,2,4,5,16,256]{5,4,3,2,1,0:T(8,128)(2,1)} collective-permute-done((bf16[1,2,4,5,16,256]{5,4,3,2,1,0:T(8,128)(2,1)}, bf16[1,2,4,5,16,256]{5,4,3,2,1,0:T(8,128)(2,1)}, u32[]{:S(2)}, u32[]{:S(2)}) %collective-permute-start.8) | collective-permute-done | bytes 327712 | tf_op jit(solution)/shard_map/ppermute | solution.py:42
  115.6 3.8 %mixgrad.1 = (bf16[256,1024]{1,0:T(8,128)(2,1)S(1)}, bf16[64,1024]{1,0:T(8,128)(2,1)S(1)}, bf16[64,1024]{1,0:T(8,128)(2,1)S(1)}) custom-call(s32[24]{0:T(128)S(1)} %concatenate.4.meta, bf16[8,2,128,512]{3,2,1,0:T(8,128)(2,1)} %bitcast.32, bf16[8,2,128,512]{3,2,1,0:T(8,128)(2,1)} %collective-permute-done.other, ...), custom_call_target="tpu_custom_call" | custom-call | flops 671088640 | bytes 7340032 | tf_op jit(solution)/shard_map/mixgrad/pallas_call | solution.py:138
  122.2 4.8 %preact.1 = (f32[256,1024]{1,0:T(8,128)}, bf16[256,1024]{1,0:T(8,128)(2,1)S(1)}, bf16[64,1024]{1,0:T(8,128)(2,1)S(1)}, bf16[64,1024]{1,0:T(8,128)(2,1)S(1)}) custom-call(s32[24]{0:T(128)S(1)} %concatenate.4.meta, bf16[8,2,128,512]{3,2,1,0:T(8,128)(2,1)} %bitcast.33, bf16[8,2,128,512]{3,2,1,0:T(8,128)(2,1)} %collective-permute-done.other, ...), custom_call_target="tpu_custom_call" | custom-call | flops 671088640 | bytes 7340032 | tf_op jit(solution)/shard_map/preact/pallas_call | solution.py:138
  127.9 8.6 %gradin.1 = (bf16[4,20,16,256]{3,2,1,0:T(8,128)(2,1)S(1)}, bf16[4,20,16,256]{3,2,1,0:T(8,128)(2,1)}, bf16[4,20,16,256]{3,2,1,0:T(8,128)(2,1)}, bf16[4,20,16,256]...) custom-call(s32[24]{0:T(128)S(1)} %concatenate.4.meta, ...), custom_call_target="tpu_custom_call" | custom-call | flops 1342177280 | bytes 12582912 | tf_op jit(solution)/shard_map/gradin/pallas_call | solution.py:292
  136.5 3.1 %collective-permute-start.12 = (bf16[16,128,256]{2,1,0:T(8,128)(2,1)}, bf16[16,128,256]{2,1,0:T(8,128)(2,1)S(1)}, u32[]{:S(2)}, u32[]{:S(2)}) collective-permute-start(bf16[16,128,256]{2,1,0:T(8,128)(2,1)} %get-tuple-element.39), channel_id=1, source_target_pairs={{0,8},{8,0},{16,24},{24,16},{32,40},{40,32},{48,56},{56,48},{64,72... | collective-permute-start | bytes 3145736 | tf_op jit(solution)/shard_map/ppermute | solution.py:37
  139.6 2.5 %collective-permute-done.12 = bf16[16,128,256]{2,1,0:T(8,128)(2,1)S(1)} collective-permute-done((bf16[16,128,256]{2,1,0:T(8,128)(2,1)}, bf16[16,128,256]{2,1,0:T(8,128)(2,1)S(1)}, u32[]{:S(2)}, u32[]{:S(2)}) %collective-permute-start.12) | collective-permute-done | bytes 1048608 | tf_op jit(solution)/shard_map/ppermute | solution.py:37
  142.1 2.7 %add_convert_fusion = bf16[16,128,256]{2,1,0:T(8,128)(2,1)} fusion(bf16[16,128,256]{2,1,0:T(8,128)(2,1)S(1)} %collective-permute-done.12, bf16[16,128,256]{2,1,0:T(8,128)(2,1)} %get-tuple-element.38), kind=kLoop, calls=%fused_computation | loop fusion | flops 2097152 | bytes 3145728 | tf_op jit(solution)/shard_map/convert_element_type | solution.py:448
  144.8 6.5 %collective-permute-start.21 = (bf16[4,20,16,256]{3,2,1,0:T(8,128)(2,1)}, bf16[4,20,16,256]{3,2,1,0:T(8,128)(2,1)S(1)}, u32[]{:S(2)}, u32[]{:S(2)}) collective-permute-start(bf16[4,20,16,256]{3,2,1,0:T(8,128)(2,1)} %get-tuple-element.52), channel_id=1, source_target_pairs={{0,64},{8,72},{16,80},{24,88},{32,96},{40,104},{48,112},{56,120},{... | collective-permute-start | bytes 1966088 | tf_op jit(solution)/shard_map/ppermute | solution.py:42
  153.9 4.0 %collective-permute-start.22 = (bf16[4,20,16,256]{3,2,1,0:T(8,128)(2,1)}, bf16[4,20,16,256]{3,2,1,0:T(8,128)(2,1)S(1)}, u32[]{:S(2)}, u32[]{:S(2)}) collective-permute-start(bf16[4,20,16,256]{3,2,1,0:T(8,128)(2,1)} %get-tuple-element.53), channel_id=1, source_target_pairs={{0,192},{8,200},{16,208},{24,216},{32,224},{40,232},{48,240},{56,2... | collective-permute-start | bytes 1966088 | tf_op jit(solution)/shard_map/ppermute | solution.py:42
  157.9 2.7 %collective-permute-start.23 = (bf16[4,20,16,256]{3,2,1,0:T(8,128)(2,1)}, bf16[4,20,16,256]{3,2,1,0:T(8,128)(2,1)S(1)}, u32[]{:S(2)}, u32[]{:S(2)}) collective-permute-start(bf16[4,20,16,256]{3,2,1,0:T(8,128)(2,1)} %get-tuple-element.54), channel_id=1, source_target_pairs={{0,128},{8,136},{16,144},{24,152},{32,160},{40,168},{48,176},{56,1... | collective-permute-start | bytes 1966088 | tf_op jit(solution)/shard_map/ppermute | solution.py:42
  160.6 5.4 %gradout.1 = (bf16[4,21,16,256]{3,2,1,0:T(8,128)(2,1)S(1)}, bf16[4,21,16,256]{3,2,1,0:T(8,128)(2,1)S(1)}, bf16[4,21,16,256]{3,2,1,0:T(8,128)(2,1)S(1)}, bf16[4,21,16,256]{3,2,1,0:T(8,128)(2,1)S(1)}) custom-call(s32[24]{0:T(128)S(1)} %concatenate.4.meta, bf16[8,2,128,512]{3,2,1,0:T(8,128)(2,1)} %bitcast.35, ...), custom_call_target="tpu_custom_call" | custom-call | flops 671088640 | bytes 7340032 | tf_op jit(solution)/shard_map/gradout/pallas_call | solution.py:221
  166.1 3.5 %collective-permute-start.16 = (bf16[4,21,16,256]{3,2,1,0:T(8,128)(2,1)S(1)}, bf16[4,21,16,256]{3,2,1,0:T(8,128)(2,1)S(1)}, u32[]{:S(2)}, u32[]{:S(2)}) collective-permute-start(bf16[4,21,16,256]{3,2,1,0:T(8,128)(2,1)S(1)} %get-tuple-element.45), channel_id=1, source_target_pairs={{0,48},{8,56},{16,0},{24,8},{32,16},{40,24},{48,32},{56,40},{64,11... | collective-permute-start | bytes 2064392 | tf_op jit(solution)/shard_map/ppermute | solution.py:33
  169.6 13.1 %collective-permute-start.17 = (bf16[4,21,16,256]{3,2,1,0:T(8,128)(2,1)S(1)}, bf16[4,21,16,256]{3,2,1,0:T(8,128)(2,1)S(1)}, u32[]{:S(2)}, u32[]{:S(2)}) collective-permute-start(bf16[4,21,16,256]{3,2,1,0:T(8,128)(2,1)S(1)} %get-tuple-element.46), channel_id=1, source_target_pairs={{0,32},{8,40},{16,48},{24,56},{32,0},{40,8},{48,16},{56,24},{64,96... | collective-permute-start | bytes 2064392 | tf_op jit(solution)/shard_map/ppermute | solution.py:33
  184.9 14.4 %collective-permute-done.17.f = bf16[4,21,16,256]{3,2,1,0:T(8,128)(2,1)S(1)} collective-permute-done((bf16[4,21,16,256]{3,2,1,0:T(8,128)(2,1)S(1)}, bf16[4,21,16,256]{3,2,1,0:T(8,128)(2,1)S(1)}, u32[]{:S(2)}, u32[]{:S(2)}) %collective-permute-start.17) | collective-permute-done | bytes 688160 | tf_op jit(solution)/shard_map/ppermute | solution.py:33
  200.4 2.7 %collective-permute-start.19 = (bf16[4,6,16,256]{3,2,1,0:T(8,128)(2,1)S(1)}, bf16[4,6,16,256]{3,2,1,0:T(8,128)(2,1)S(1)}, u32[]{:S(2)}, u32[]{:S(2)}) collective-permute-start(bf16[4,6,16,256]{3,2,1,0:T(8,128)(2,1)S(1)} %get-tuple-element.49), channel_id=1, source_target_pairs={{0,192},{8,200},{16,208},{24,216},{32,224},{40,232},{48,240},{56,2... | collective-permute-start | bytes 589832 | tf_op jit(solution)/shard_map/ppermute | solution.py:42
  207.2 2.8 %collective-permute-done.26.refs_7_ = bf16[4,5,16,256]{3,2,1,0:T(8,128)(2,1)S(1)} collective-permute-done((bf16[4,5,16,256]{3,2,1,0:T(8,128)(2,1)S(1)}, bf16[4,5,16,256]{3,2,1,0:T(8,128)(2,1)S(1)}, u32[]{:S(2)}, u32[]{:S(2)}) %collective-permute-start.26) | collective-permute-done | bytes 163872 | tf_op jit(solution)/shard_map/ppermute | solution.py:33
  211.2 4.7 %collective-permute-start.27 = (bf16[2,4,6,8,256]{4,3,2,1,0:T(8,128)(2,1)S(1)}, bf16[2,4,6,8,256]{4,3,2,1,0:T(8,128)(2,1)S(1)}, u32[]{:S(2)}, u32[]{:S(2)}) collective-permute-start(bf16[2,4,6,8,256]{4,3,2,1,0:T(8,128)(2,1)S(1)} %get-tuple-element.60), channel_id=1, source_target_pairs={{0,8},{8,0},{16,24},{24,16},{32,40},{40,32},{48,56},{56,48},{64,72... | collective-permute-start | bytes 589832 | tf_op jit(solution)/shard_map/ppermute | solution.py:37
  (79 shorter events, 30.0 us)
Async XLA Ops:
  7.2 44.4 %all-gather.3.cloned.1.call-start = ((), (), s32[]{:S(2)}) async-start(), calls=%async_computation.2 | async-start | bytes 2359296 | tf_op jit(solution)/shard_map/all_gather | solution.py:422
  8.9 209.6 %reduce-scatter.2.cloned.1.call-start = ((), (), s32[]{:S(2)}) async-start(), calls=%async_computation.1 | async-start | bytes 1179648 | tf_op jit(solution)/shard_map/reduce_scatter | solution.py:449
  51.6 64.0 %collective-permute-start = (bf16[8,2,128,512]{3,2,1,0:T(8,128)(2,1)}, bf16[8,2,128,512]{3,2,1,0:T(8,128)(2,1)}, u32[]{:S(2)}, u32[]{:S(2)}) collective-permute-start(bf16[8,2,128,512]{3,2,1,0:T(8,128)(2,1)} %bitcast.31), channel_id=1, source_target_pairs={{0,8},{8,0},{16,24},{24,16},{32,40},{40,32},{48,56},{56,48},{64,72... | collective-permute-start | bytes 6291464 | tf_op jit(solution)/shard_map/ppermute | solution.py:37
  60.3 30.4 %collective-permute-start.3 = (bf16[2,2,4,5,16,256]{5,4,3,2,1,0:T(8,128)(2,1)S(1)}, bf16[2,2,4,5,16,256]{5,4,3,2,1,0:T(8,128)(2,1)S(1)}, u32[]{:S(2)}, u32[]{:S(2)}) collective-permute-start(bf16[2,2,4,5,16,256]{5,4,3,2,1,0:T(8,128)(2,1)S(1)} %pad_maximum_fusion.refs_0_), channel_id=1, source_target_pairs={{0,48},{8,56},{16,0},{24,8},{32,16},{40,24},{48,32},{56,40},{64,11... | collective-permute-start | bytes 1966088 | tf_op jit(solution)/shard_map/ppermute | solution.py:33
  62.7 30.4 %collective-permute-start.2 = (bf16[2,2,4,5,16,256]{5,4,3,2,1,0:T(8,128)(2,1)S(1)}, bf16[2,2,4,5,16,256]{5,4,3,2,1,0:T(8,128)(2,1)S(1)}, u32[]{:S(2)}, u32[]{:S(2)}) collective-permute-start(bf16[2,2,4,5,16,256]{5,4,3,2,1,0:T(8,128)(2,1)S(1)} %pad_maximum_fusion.refs_0_), channel_id=1, source_target_pairs={{0,16},{8,24},{16,32},{24,40},{32,48},{40,56},{48,0},{56,8},{64,80... | collective-permute-start | bytes 1966088 | tf_op jit(solution)/shard_map/ppermute | solution.py:33
  62.7 30.4 %collective-permute-start.4 = (bf16[2,2,4,5,16,256]{5,4,3,2,1,0:T(8,128)(2,1)S(1)}, bf16[2,2,4,5,16,256]{5,4,3,2,1,0:T(8,128)(2,1)S(1)}, u32[]{:S(2)}, u32[]{:S(2)}) collective-permute-start(bf16[2,2,4,5,16,256]{5,4,3,2,1,0:T(8,128)(2,1)S(1)} %pad_maximum_fusion.refs_0_), channel_id=1, source_target_pairs={{0,32},{8,40},{16,48},{24,56},{32,0},{40,8},{48,16},{56,24},{64,96... | collective-permute-start | bytes 1966088 | tf_op jit(solution)/shard_map/ppermute | solution.py:33
  64.5 32.3 %collective-permute-start.5 = (bf16[2,2,4,5,16,256]{5,4,3,2,1,0:T(8,128)(2,1)S(1)}, bf16[2,2,4,5,16,256]{5,4,3,2,1,0:T(8,128)(2,1)S(1)}, u32[]{:S(2)}, u32[]{:S(2)}) collective-permute-start(bf16[2,2,4,5,16,256]{5,4,3,2,1,0:T(8,128)(2,1)S(1)} %pad_maximum_fusion.refs_0_), channel_id=1, source_target_pairs={{0,64},{8,72},{16,80},{24,88},{32,96},{40,104},{48,112},{56,120},{... | collective-permute-start | bytes 1966088 | tf_op jit(solution)/shard_map/ppermute | solution.py:42
  90.6 25.0 %collective-permute-start.7 = (bf16[2,2,4,5,16,256]{5,4,3,2,1,0:T(8,128)(2,1)S(1)}, bf16[2,2,4,5,16,256]{5,4,3,2,1,0:T(8,128)(2,1)}, u32[]{:S(2)}, u32[]{:S(2)}) collective-permute-start(bf16[2,2,4,5,16,256]{5,4,3,2,1,0:T(8,128)(2,1)S(1)} %collective-permute-done.3.refs_2_), channel_id=1, source_target_pairs={{0,192},{8,200},{16,208},{24,216},{32,224},{40,232},{48,240},{56,2... | collective-permute-start | bytes 1966088 | tf_op jit(solution)/shard_map/ppermute | solution.py:42
  93.1 22.5 %collective-permute-start.6 = (bf16[2,2,4,5,16,256]{5,4,3,2,1,0:T(8,128)(2,1)S(1)}, bf16[2,2,4,5,16,256]{5,4,3,2,1,0:T(8,128)(2,1)}, u32[]{:S(2)}, u32[]{:S(2)}) collective-permute-start(bf16[2,2,4,5,16,256]{5,4,3,2,1,0:T(8,128)(2,1)S(1)} %collective-permute-done.2.refs_1_), channel_id=1, source_target_pairs={{0,64},{8,72},{16,80},{24,88},{32,96},{40,104},{48,112},{56,120},{... | collective-permute-start | bytes 1966088 | tf_op jit(solution)/shard_map/ppermute | solution.py:42
  94.1 19.0 %collective-permute-start.9 = (bf16[1,2,4,5,16,256]{5,4,3,2,1,0:T(8,128)(2,1)}, bf16[1,2,4,5,16,256]{5,4,3,2,1,0:T(8,128)(2,1)}, u32[]{:S(2)}, u32[]{:S(2)}) collective-permute-start(bf16[1,2,4,5,16,256]{5,4,3,2,1,0:T(8,128)(2,1)} %get-tuple-element.66), channel_id=1, source_target_pairs={{0,192},{8,200},{16,208},{24,216},{32,224},{40,232},{48,240},{56,2... | collective-permute-start | bytes 983048 | tf_op jit(solution)/shard_map/ppermute | solution.py:42
  96.8 18.8 %collective-permute-start.8 = (bf16[1,2,4,5,16,256]{5,4,3,2,1,0:T(8,128)(2,1)}, bf16[1,2,4,5,16,256]{5,4,3,2,1,0:T(8,128)(2,1)}, u32[]{:S(2)}, u32[]{:S(2)}) collective-permute-start(bf16[1,2,4,5,16,256]{5,4,3,2,1,0:T(8,128)(2,1)} %get-tuple-element.67), channel_id=1, source_target_pairs={{0,64},{8,72},{16,80},{24,88},{32,96},{40,104},{48,112},{56,120},{... | collective-permute-start | bytes 983048 | tf_op jit(solution)/shard_map/ppermute | solution.py:42
  119.5 8.4 %collective-permute-start.10 = (bf16[64,1024]{1,0:T(8,128)(2,1)S(1)}, bf16[64,1024]{1,0:T(8,128)(2,1)S(1)}, u32[]{:S(2)}, u32[]{:S(2)}) collective-permute-start(bf16[64,1024]{1,0:T(8,128)(2,1)S(1)} %get-tuple-element.36), channel_id=1, source_target_pairs={{0,16},{8,24},{16,32},{24,40},{32,48},{40,56},{48,64},{56,72},{64,... | collective-permute-start | bytes 393224 | tf_op jit(solution)/shard_map/ppermute | solution.py:50
  144.8 24.8 %collective-permute-start.21 = (bf16[4,20,16,256]{3,2,1,0:T(8,128)(2,1)}, bf16[4,20,16,256]{3,2,1,0:T(8,128)(2,1)S(1)}, u32[]{:S(2)}, u32[]{:S(2)}) collective-permute-start(bf16[4,20,16,256]{3,2,1,0:T(8,128)(2,1)} %get-tuple-element.52), channel_id=1, source_target_pairs={{0,64},{8,72},{16,80},{24,88},{32,96},{40,104},{48,112},{56,120},{... | collective-permute-start | bytes 1966088 | tf_op jit(solution)/shard_map/ppermute | solution.py:42
  151.3 9.3 %collective-permute-start.13 = (bf16[64,1024]{1,0:T(8,128)(2,1)S(1)}, bf16[64,1024]{1,0:T(8,128)(2,1)S(1)}, u32[]{:S(2)}, u32[]{:S(2)}) collective-permute-start(bf16[64,1024]{1,0:T(8,128)(2,1)S(1)} %copy-done.9), channel_id=1, source_target_pairs={{0,16},{8,24},{16,32},{24,40},{32,48},{40,56},{48,64},{56,72},{64,... | collective-permute-start | bytes 393224 | tf_op jit(solution)/shard_map/ppermute | solution.py:50
  152.6 8.0 %collective-permute-start.14 = (bf16[64,1024]{1,0:T(8,128)(2,1)S(1)}, bf16[64,1024]{1,0:T(8,128)(2,1)S(1)}, u32[]{:S(2)}, u32[]{:S(2)}) collective-permute-start(bf16[64,1024]{1,0:T(8,128)(2,1)S(1)} %get-tuple-element.42), channel_id=1, source_target_pairs={{16,0},{24,8},{32,16},{40,24},{48,32},{56,40},{64,48},{72,56},{80,... | collective-permute-start | bytes 393224 | tf_op jit(solution)/shard_map/ppermute | solution.py:50
  153.9 28.8 %collective-permute-start.22 = (bf16[4,20,16,256]{3,2,1,0:T(8,128)(2,1)}, bf16[4,20,16,256]{3,2,1,0:T(8,128)(2,1)S(1)}, u32[]{:S(2)}, u32[]{:S(2)}) collective-permute-start(bf16[4,20,16,256]{3,2,1,0:T(8,128)(2,1)} %get-tuple-element.53), channel_id=1, source_target_pairs={{0,192},{8,200},{16,208},{24,216},{32,224},{40,232},{48,240},{56,2... | collective-permute-start | bytes 1966088 | tf_op jit(solution)/shard_map/ppermute | solution.py:42
  157.9 25.2 %collective-permute-start.23 = (bf16[4,20,16,256]{3,2,1,0:T(8,128)(2,1)}, bf16[4,20,16,256]{3,2,1,0:T(8,128)(2,1)S(1)}, u32[]{:S(2)}, u32[]{:S(2)}) collective-permute-start(bf16[4,20,16,256]{3,2,1,0:T(8,128)(2,1)} %get-tuple-element.54), channel_id=1, source_target_pairs={{0,128},{8,136},{16,144},{24,152},{32,160},{40,168},{48,176},{56,1... | collective-permute-start | bytes 1966088 | tf_op jit(solution)/shard_map/ppermute | solution.py:42
  166.0 18.9 %collective-permute-start.15 = (bf16[4,21,16,256]{3,2,1,0:T(8,128)(2,1)S(1)}, bf16[4,21,16,256]{3,2,1,0:T(8,128)(2,1)S(1)}, u32[]{:S(2)}, u32[]{:S(2)}) collective-permute-start(bf16[4,21,16,256]{3,2,1,0:T(8,128)(2,1)S(1)} %get-tuple-element.44), channel_id=1, source_target_pairs={{0,16},{8,24},{16,32},{24,40},{32,48},{40,56},{48,0},{56,8},{64,80... | collective-permute-start | bytes 2064392 | tf_op jit(solution)/shard_map/ppermute | solution.py:33
  166.1 18.8 %collective-permute-start.16 = (bf16[4,21,16,256]{3,2,1,0:T(8,128)(2,1)S(1)}, bf16[4,21,16,256]{3,2,1,0:T(8,128)(2,1)S(1)}, u32[]{:S(2)}, u32[]{:S(2)}) collective-permute-start(bf16[4,21,16,256]{3,2,1,0:T(8,128)(2,1)S(1)} %get-tuple-element.45), channel_id=1, source_target_pairs={{0,48},{8,56},{16,0},{24,8},{32,16},{40,24},{48,32},{56,40},{64,11... | collective-permute-start | bytes 2064392 | tf_op jit(solution)/shard_map/ppermute | solution.py:33
  169.6 29.7 %collective-permute-start.17 = (bf16[4,21,16,256]{3,2,1,0:T(8,128)(2,1)S(1)}, bf16[4,21,16,256]{3,2,1,0:T(8,128)(2,1)S(1)}, u32[]{:S(2)}, u32[]{:S(2)}) collective-permute-start(bf16[4,21,16,256]{3,2,1,0:T(8,128)(2,1)S(1)} %get-tuple-element.46), channel_id=1, source_target_pairs={{0,32},{8,40},{16,48},{24,56},{32,0},{40,8},{48,16},{56,24},{64,96... | collective-permute-start | bytes 2064392 | tf_op jit(solution)/shard_map/ppermute | solution.py:33
  184.1 20.2 %collective-permute-start.24 = (bf16[4,5,16,256]{3,2,1,0:T(8,128)(2,1)S(1)}, bf16[4,5,16,256]{3,2,1,0:T(8,128)(2,1)S(1)}, u32[]{:S(2)}, u32[]{:S(2)}) collective-permute-start(bf16[4,5,16,256]{3,2,1,0:T(8,128)(2,1)S(1)} %get-tuple-element.56), channel_id=1, source_target_pairs={{0,16},{8,24},{16,32},{24,40},{32,48},{40,56},{48,0},{56,8},{64,80... | collective-permute-start | bytes 491528 | tf_op jit(solution)/shard_map/ppermute | solution.py:33
  200.3 9.7 %collective-permute-start.18 = (bf16[4,6,16,256]{3,2,1,0:T(8,128)(2,1)S(1)}, bf16[4,6,16,256]{3,2,1,0:T(8,128)(2,1)S(1)}, u32[]{:S(2)}, u32[]{:S(2)}) collective-permute-start(bf16[4,6,16,256]{3,2,1,0:T(8,128)(2,1)S(1)} %get-tuple-element.48), channel_id=1, source_target_pairs={{0,64},{8,72},{16,80},{24,88},{32,96},{40,104},{48,112},{56,120},{... | collective-permute-start | bytes 589832 | tf_op jit(solution)/shard_map/ppermute | solution.py:42
  200.4 9.6 %collective-permute-start.19 = (bf16[4,6,16,256]{3,2,1,0:T(8,128)(2,1)S(1)}, bf16[4,6,16,256]{3,2,1,0:T(8,128)(2,1)S(1)}, u32[]{:S(2)}, u32[]{:S(2)}) collective-permute-start(bf16[4,6,16,256]{3,2,1,0:T(8,128)(2,1)S(1)} %get-tuple-element.49), channel_id=1, source_target_pairs={{0,192},{8,200},{16,208},{24,216},{32,224},{40,232},{48,240},{56,2... | collective-permute-start | bytes 589832 | tf_op jit(solution)/shard_map/ppermute | solution.py:42
  203.0 7.4 %collective-permute-start.20 = (bf16[4,6,16,256]{3,2,1,0:T(8,128)(2,1)S(1)}, bf16[4,6,16,256]{3,2,1,0:T(8,128)(2,1)S(1)}, u32[]{:S(2)}, u32[]{:S(2)}) collective-permute-start(bf16[4,6,16,256]{3,2,1,0:T(8,128)(2,1)S(1)} %get-tuple-element.50), channel_id=1, source_target_pairs={{0,128},{8,136},{16,144},{24,152},{32,160},{40,168},{48,176},{56,1... | collective-permute-start | bytes 589832 | tf_op jit(solution)/shard_map/ppermute | solution.py:42
  (16 other events, 247.8 us)
Sparse Core Ops, SparseCore 0:
  10.4 41.1 all-gather.2
  144.9 34.3 reduce-scatter.1

commit v2 on v1

--- a/solution.py
+++ b/solution.py
@@ -58,6 +58,17 @@
     return pltpu.CompilerParams(dimension_semantics=("arbitrary",), vmem_limit_bytes=48 * 2**20)
 
 
+def after(value, *others):
+    return pl.pallas_call(
+        lambda *refs: None,
+        out_shape=jax.ShapeDtypeStruct(value.shape, value.dtype),
+        in_specs=[ANY] * (1 + len(others)),
+        out_specs=ANY,
+        input_output_aliases={0: 0},
+        name="after",
+    )(value, *others)
+
+
 def start_tokens(meta, own, other, which, buf, sem):
     core = meta[CORE]
     for src, at in ((own, core), (other, 1 - core)):
@@ -74,7 +85,7 @@
 
 def start_weights(meta, pieces, which, buf, sems):
     x, ylo = meta[XPOS], meta[YLO]
-    own, xm, xp, x2, yo, ym, yp, y2a, y2b = pieces
+    own, xm, xp, x2a, x2b, yo, ym, yp, y2a, y2b = pieces
     here, there = ylo * NX, (1 - ylo) * NX
     at = lambda base, d: base + (x + d) % NX
     plan = []
@@ -83,12 +94,12 @@
             (own, s, at(here, 0), s),
             (xm, s, at(here, 3), s),
             (xp, s, at(here, 1), s),
-            (x2, s, at(here, 2), s),
             (yo, s, at(there, 0), s),
             (ym, s, at(there, 3), s),
             (yp, s, at(there, 1), s),
         ]
-    plan += [(y2a, 0, at(there, 2), 0), (y2b, 0, at(there, 2), 1)]
+    for base, a, b in ((here, x2a, x2b), (there, y2a, y2b)):
+        plan += [(a, 0, at(base, 2), 0), (b, 0, at(base, 2), 1)]
     for c in range(COLS):
         for src, row, j, s in plan:
             pltpu.make_async_copy(src.at[row, which, c], buf.at[c, :, 2 * j + s], sems.at[c]).start()
@@ -99,7 +110,7 @@
 
 
 def forward_kernel(which, meta, own, other, *refs):
-    pieces, refs = refs[:9], refs[9:]
+    pieces, refs = refs[:10], refs[10:]
     if which == 0:
         pre_ref, act_ref, top_ref, bot_ref, tok, wts, tok_sem, w_sems = refs
     else:
@@ -141,7 +152,7 @@
         grid_spec=pltpu.PrefetchScalarGridSpec(
             num_scalar_prefetch=1,
             grid=(COLS,),
-            in_specs=[ANY] * 11,
+            in_specs=[ANY] * 12,
             out_specs=[column(r) for r, _ in outs],
             scratch_shapes=[
                 pltpu.VMEM((8, 2, TOK, BS), BF16),
@@ -242,9 +253,9 @@
 
 
 def grad_in_kernel(meta, own, other, *refs):
-    pieces, refs = refs[:9], refs[9:]
-    pre, mgrad, up, down, taps = refs[:5]
-    outs, (keep, send, tok, wts, pgrad, res, acc, sem, w_sems) = refs[5 : 5 + NY], refs[5 + NY :]
+    pieces, refs = refs[:10], refs[10:]
+    _, pre, mgrad, up, down, taps = refs[:6]
+    outs, (keep, send, tok, wts, pgrad, res, acc, sem, w_sems) = refs[6 : 6 + NY], refs[6 + NY :]
     c = pl.program_id(0)
     core, y_here = meta[CORE], meta[YPOS]
 
@@ -287,7 +298,7 @@
         send[...] = acc[:, pl.ds(pl.multiple_of((1 - core) * 128, 128), 128)].astype(BF16)
 
 
-def grad_in(meta, own, other, pieces, pre, mgrad, up, down, taps):
+def grad_in(meta, own, other, pieces, after, pre, mgrad, up, down, taps):
     half = pl.BlockSpec((16, 128, BS), lambda c, m: (0, 0, 0))
     return pl.pallas_call(
         grad_in_kernel,
@@ -296,7 +307,7 @@
         grid_spec=pltpu.PrefetchScalarGridSpec(
             num_scalar_prefetch=1,
             grid=(COLS,),
-            in_specs=[ANY] * 11 + [column(TOK), column(TOK), column(PW), column(PW), taps_spec()],
+            in_specs=[ANY] * 13 + [column(TOK), column(TOK), column(PW), column(PW), taps_spec()],
             out_specs=[slabs(20)] * NY + [half, half],
             scratch_shapes=[
                 pltpu.VMEM((8, 2, TOK, BS), BF16),
@@ -313,7 +324,7 @@
             flops=4 * TOK * BS * BS * NNZ * COLS, transcendentals=TOK * BS * COLS, bytes_accessed=12 * 2**20
         ),
         name="gradin",
-    )(meta, own, other, *pieces, pre, mgrad, up, down, taps)
+    )(meta, own, other, *pieces, after, pre, mgrad, up, down, taps)
 
 
 def first_sum_kernel(pos, extra, meta, a, b, e, f, *outs):
@@ -429,11 +440,12 @@
     piece = jnp.stack([jnp.where(core == 0, mine, got), jnp.where(core == 0, got, mine)])
     xm, xp = along_x(piece, 1), along_x(piece, -1)
     yo = along_y(piece, 1)
-    x2 = along_x(piece, 2)
     ym, yp = along_y(xm, 1), along_y(xp, -1)
-    y2a, y2b = along_y(x2[:1], 1), along_y(x2[1:], -1)
-    pieces = (piece, xm, xp, x2, yo, ym, yp, y2a, y2b)
-
+    x2a, x2b = along_x(xm[:1], 1), along_x(xp[1:], -1)
+    y2a, y2b = along_y(x2a, 1), along_y(x2b, -1)
+    pieces = (piece, xm, xp, x2a, x2b, yo, ym, yp, y2a, y2b)
+
+    own = after(own, y2a, y2b)
     other = to_partner(own)
     pre, act, act_top, act_bot = forward(0, meta, own, other, pieces)
     act_up, act_down = to_next_chip(act_bot, 1), to_next_chip(act_top, -1)
@@ -442,7 +454,7 @@
 
     outs = grad_out(meta, own, other, act, act_up, act_down, mgrad, mix_kernel)
     a_parts = (outs[0], along_x(outs[1], 1), along_x(outs[3], -1), along_x(outs[2], 2))
-    *ins, keep, send = grad_in(meta, own, other, pieces, pre, mgrad, mg_up, mg_down, mix_kernel)
+    *ins, keep, send = grad_in(meta, own, other, pieces, outs[0], pre, mgrad, mg_up, mg_down, mix_kernel)
     b_parts = (ins[0], along_y(ins[1], 1), along_y(ins[3], -1), along_y(ins[2], 2))
 
     terms = (keep.astype(F32) + to_partner(send).astype(F32)).astype(BF16)

time: 228 us -> 214 us (0.939)
  the two profiles are of different devices: /device:TPU:1 before, /device:TPU:145 now
where the time goes in v2:
time: 214 us; the launch traced here: 213 us
  waiting for transfers between devices  93.6 us (44%)
  starting transfers between devices  59.9 us (28%)
  Pallas kernels  26.6 us (12%)
  local copies, waits for them, and re-layouts  14.5 us (7%)
  between operations  14.4 us (7%)
  other arithmetic  4.47 us (2%)
    ppermute x11, waiting for transfers between devices, along_y(): return lax.ppermute(value, ('crop', 'rows'), pairs)  58.5 us
    ppermute x10, waiting for transfers between devices, along_x(): lax.ppermute(value, 'rows', row_perm(lambda y, x, c: (y, x + step, c)))  30.2 us
    ppermute x11, starting transfers between devices, along_y(): return lax.ppermute(value, ('crop', 'rows'), pairs)  29.6 us
    unnamed x52, local copies, waits for them, and re-layouts  12.5 us
    ppermute x10, starting transfers between devices, along_x(): lax.ppermute(value, 'rows', row_perm(lambda y, x, c: (y, x + step, c)))  12.2 us
    ppermute x4, starting transfers between devices, to_partner(): return lax.ppermute(value, 'rows', row_perm(lambda y, x, c: (y, x, 1 - c)))  9.89 us
    pallas_call x2, Pallas kernels, forward(): pl.pallas_call(functools.partial(forward_kernel, which), out_shape=[jax.S...  8.61 us
    pallas_call x1, Pallas kernels, grad_in(): pl.pallas_call(grad_in_kernel, out_shape=[jax.ShapeDtypeStruct((COLS, 20,...  8.45 us
  transfers between devices with their start and end apart: 31, of which 16 were waited for; matrix products, arithmetic and copies ran while one was open for 1% of the time, Pallas kernels for 6%

profile of v2, /device:TPU:145, one launch (start us, length us, event | category | flops | bytes accessed | tf_op | source)
XLA Modules:
  0.0 213.5 jit_solution(13723256269356458953)
XLA Ops:
  13.3 2.6 %collective-permute-start.4 = (bf16[2,2,4,5,16,256]{5,4,3,2,1,0:T(8,128)(2,1)S(1)}, bf16[2,2,4,5,16,256]{5,4,3,2,1,0:T(8,128)(2,1)S(1)}, u32[]{:S(2)}, u32[]{:S(2)}) collective-permute-start(bf16[2,2,4,5,16,256]{5,4,3,2,1,0:T(8,128)(2,1)S(1)} %pad_maximum_fusion.refs_0_), channel_id=1, source_target_pairs={{0,48},{8,56},{16,0},{24,8},{32,16},{40,24},{48,32},{56,40},{64,11... | collective-permute-start | bytes 1966088 | tf_op jit(solution)/shard_map/ppermute | solution.py:33
  15.8 13.7 %collective-permute-done.4.refs_2_ = bf16[2,2,4,5,16,256]{5,4,3,2,1,0:T(8,128)(2,1)S(1)} collective-permute-done((bf16[2,2,4,5,16,256]{5,4,3,2,1,0:T(8,128)(2,1)S(1)}, bf16[2,2,4,5,16,256]{5,4,3,2,1,0:T(8,128)(2,1)S(1)}, u32[]{:S(2)}, u32[]{:S(2)}) %collective-permute-start.4) | collective-permute-done | bytes 655392 | tf_op jit(solution)/shard_map/ppermute | solution.py:33
  29.6 3.5 %collective-permute-start.5 = (bf16[1,2,4,5,16,256]{5,4,3,2,1,0:T(8,128)(2,1)S(1)}, bf16[1,2,4,5,16,256]{5,4,3,2,1,0:T(8,128)(2,1)S(1)}, u32[]{:S(2)}, u32[]{:S(2)}) collective-permute-start(bf16[1,2,4,5,16,256]{5,4,3,2,1,0:T(8,128)(2,1)S(1)} %slice.9), channel_id=1, source_target_pairs={{0,48},{8,56},{16,0},{24,8},{32,16},{40,24},{48,32},{56,40},{64,11... | collective-permute-start | bytes 983048 | tf_op jit(solution)/shard_map/ppermute | solution.py:33
  33.2 5.7 %collective-permute-done.5.refs_4_ = bf16[1,2,4,5,16,256]{5,4,3,2,1,0:T(8,128)(2,1)S(1)} collective-permute-done((bf16[1,2,4,5,16,256]{5,4,3,2,1,0:T(8,128)(2,1)S(1)}, bf16[1,2,4,5,16,256]{5,4,3,2,1,0:T(8,128)(2,1)S(1)}, u32[]{:S(2)}, u32[]{:S(2)}) %collective-permute-start.5) | collective-permute-done | bytes 327712 | tf_op jit(solution)/shard_map/ppermute | solution.py:33
  46.1 3.0 %collective-permute-done.3.refs_1_.refs_8_ = bf16[1,2,4,5,16,256]{5,4,3,2,1,0:T(8,128)(2,1)S(1)} collective-permute-done((bf16[1,2,4,5,16,256]{5,4,3,2,1,0:T(8,128)(2,1)S(1)}, bf16[1,2,4,5,16,256]{5,4,3,2,1,0:T(8,128)(2,1)S(1)}, u32[]{:S(2)}, u32[]{:S(2)}) %collective-permute-start.3) | collective-permute-done | bytes 327712 | tf_op jit(solution)/shard_map/ppermute | solution.py:42
  49.8 3.2 %collective-permute-start.7 = (bf16[8,2,128,512]{3,2,1,0:T(8,128)(2,1)}, bf16[8,2,128,512]{3,2,1,0:T(8,128)(2,1)}, u32[]{:S(2)}, u32[]{:S(2)}) collective-permute-start(bf16[8,2,128,512]{3,2,1,0:T(8,128)(2,1)} %after.1.own), channel_id=1, source_target_pairs={{0,8},{8,0},{16,24},{24,16},{32,40},{40,32},{48,56},{56,48},{64,72... | collective-permute-start | bytes 6291464 | tf_op jit(solution)/shard_map/ppermute | solution.py:37
  56.0 13.4 %collective-permute-done.8.refs_5_ = bf16[2,2,4,5,16,256]{5,4,3,2,1,0:T(8,128)(2,1)S(1)} collective-permute-done((bf16[2,2,4,5,16,256]{5,4,3,2,1,0:T(8,128)(2,1)S(1)}, bf16[2,2,4,5,16,256]{5,4,3,2,1,0:T(8,128)(2,1)S(1)}, u32[]{:S(2)}, u32[]{:S(2)}) %collective-permute-start.8) | collective-permute-done | bytes 655392 | tf_op jit(solution)/shard_map/ppermute | solution.py:42
  70.5 13.0 %collective-permute-done.9.refs_6_ = bf16[2,2,4,5,16,256]{5,4,3,2,1,0:T(8,128)(2,1)} collective-permute-done((bf16[2,2,4,5,16,256]{5,4,3,2,1,0:T(8,128)(2,1)S(1)}, bf16[2,2,4,5,16,256]{5,4,3,2,1,0:T(8,128)(2,1)}, u32[]{:S(2)}, u32[]{:S(2)}) %collective-permute-start.9) | collective-permute-done | bytes 655392 | tf_op jit(solution)/shard_map/ppermute | solution.py:42
  87.4 4.8 %preact.1 = (f32[256,1024]{1,0:T(8,128)}, bf16[256,1024]{1,0:T(8,128)(2,1)S(1)}, bf16[64,1024]{1,0:T(8,128)(2,1)S(1)}, bf16[64,1024]{1,0:T(8,128)(2,1)S(1)}) custom-call(s32[24]{0:T(128)S(1)} %concatenate.4.meta, bf16[8,2,128,512]{3,2,1,0:T(8,128)(2,1)} %after.1.own, bf16[8,2,128,512]{3,2,1,0:T(8,128)(2,1)} %collective-permute-done.7.other, ...), custom_call_target="tpu_custom_call" | custom-call | flops 671088640 | bytes 7340032 | tf_op jit(solution)/shard_map/preact/pallas_call | solution.py:149
  95.0 3.8 %mixgrad.1 = (bf16[256,1024]{1,0:T(8,128)(2,1)S(1)}, bf16[64,1024]{1,0:T(8,128)(2,1)S(1)}, bf16[64,1024]{1,0:T(8,128)(2,1)S(1)}) custom-call(s32[24]{0:T(128)S(1)} %concatenate.4.meta, bf16[8,2,128,512]{3,2,1,0:T(8,128)(2,1)} %after.1.own, bf16[8,2,128,512]{3,2,1,0:T(8,128)(2,1)} %collective-permute-done.7.other, ...), custom_call_target="tpu_custom_call" | custom-call | flops 671088640 | bytes 7340032 | tf_op jit(solution)/shard_map/mixgrad/pallas_call | solution.py:149
  98.8 4.0 %collective-permute-start.13 = (bf16[64,1024]{1,0:T(8,128)(2,1)S(1)}, bf16[64,1024]{1,0:T(8,128)(2,1)S(1)}, u32[]{:S(2)}, u32[]{:S(2)}) collective-permute-start(bf16[64,1024]{1,0:T(8,128)(2,1)S(1)} %get-tuple-element.40), channel_id=1, source_target_pairs={{0,16},{8,24},{16,32},{24,40},{32,48},{40,56},{48,64},{56,72},{64,... | collective-permute-start | bytes 393224 | tf_op jit(solution)/shard_map/ppermute | solution.py:50
  104.4 5.4 %gradout.1 = (bf16[4,21,16,256]{3,2,1,0:T(8,128)(2,1)S(1)}, bf16[4,21,16,256]{3,2,1,0:T(8,128)(2,1)S(1)}, bf16[4,21,16,256]{3,2,1,0:T(8,128)(2,1)S(1)}, bf16[4,21,16,256]{3,2,1,0:T(8,128)(2,1)S(1)}) custom-call(s32[24]{0:T(128)S(1)} %concatenate.4.meta, bf16[8,2,128,512]{3,2,1,0:T(8,128)(2,1)} %after.1.own, ...), custom_call_target="tpu_custom_call" | custom-call | flops 671088640 | bytes 7340032 | tf_op jit(solution)/shard_map/gradout/pallas_call | solution.py:232
  111.6 8.4 %gradin.1 = (bf16[4,20,16,256]{3,2,1,0:T(8,128)(2,1)S(1)}, bf16[4,20,16,256]{3,2,1,0:T(8,128)(2,1)S(1)}, bf16[4,20,16,256]{3,2,1,0:T(8,128)(2,1)S(1)}, bf16[4,20...) custom-call(s32[24]{0:T(128)S(1)} %concatenate.4.meta, ...), custom_call_target="tpu_custom_call" | custom-call | flops 1342177280 | bytes 12582912 | tf_op jit(solution)/shard_map/gradin/pallas_call | solution.py:303
  126.5 2.6 %add_convert_fusion = bf16[16,128,256]{2,1,0:T(8,128)(2,1)} fusion(bf16[16,128,256]{2,1,0:T(8,128)(2,1)S(1)} %collective-permute-done.15, bf16[16,128,256]{2,1,0:T(8,128)(2,1)} %get-tuple-element.42), kind=kLoop, calls=%fused_computation | loop fusion | flops 2097152 | bytes 3145728 | tf_op jit(solution)/shard_map/convert_element_type | solution.py:460
  129.2 8.8 %collective-permute-start.22 = (bf16[4,20,16,256]{3,2,1,0:T(8,128)(2,1)}, bf16[4,20,16,256]{3,2,1,0:T(8,128)(2,1)S(1)}, u32[]{:S(2)}, u32[]{:S(2)}) collective-permute-start(bf16[4,20,16,256]{3,2,1,0:T(8,128)(2,1)} %copy-done.24), channel_id=1, source_target_pairs={{0,64},{8,72},{16,80},{24,88},{32,96},{40,104},{48,112},{56,120},{... | collective-permute-start | bytes 1966088 | tf_op jit(solution)/shard_map/ppermute | solution.py:42
  140.4 2.7 %collective-permute-start.17 = (bf16[4,21,16,256]{3,2,1,0:T(8,128)(2,1)S(1)}, bf16[4,21,16,256]{3,2,1,0:T(8,128)(2,1)S(1)}, u32[]{:S(2)}, u32[]{:S(2)}) collective-permute-start(bf16[4,21,16,256]{3,2,1,0:T(8,128)(2,1)S(1)} %get-tuple-element.45), channel_id=1, source_target_pairs={{0,48},{8,56},{16,0},{24,8},{32,16},{40,24},{48,32},{56,40},{64,11... | collective-permute-start | bytes 2064392 | tf_op jit(solution)/shard_map/ppermute | solution.py:33
  143.1 11.3 %collective-permute-done.22.b = bf16[4,20,16,256]{3,2,1,0:T(8,128)(2,1)S(1)} collective-permute-done((bf16[4,20,16,256]{3,2,1,0:T(8,128)(2,1)}, bf16[4,20,16,256]{3,2,1,0:T(8,128)(2,1)S(1)}, u32[]{:S(2)}, u32[]{:S(2)}) %collective-permute-start.22) | collective-permute-done | bytes 655392 | tf_op jit(solution)/shard_map/ppermute | solution.py:42
  154.4 14.8 %collective-permute-done.24.f = bf16[4,20,16,256]{3,2,1,0:T(8,128)(2,1)S(1)} collective-permute-done((bf16[4,20,16,256]{3,2,1,0:T(8,128)(2,1)}, bf16[4,20,16,256]{3,2,1,0:T(8,128)(2,1)S(1)}, u32[]{:S(2)}, u32[]{:S(2)}) %collective-permute-start.24) | collective-permute-done | bytes 655392 | tf_op jit(solution)/shard_map/ppermute | solution.py:42
  170.2 2.8 %collective-permute-done.18.f = bf16[4,21,16,256]{3,2,1,0:T(8,128)(2,1)S(1)} collective-permute-done((bf16[4,21,16,256]{3,2,1,0:T(8,128)(2,1)S(1)}, bf16[4,21,16,256]{3,2,1,0:T(8,128)(2,1)S(1)}, u32[]{:S(2)}, u32[]{:S(2)}) %collective-permute-start.18) | collective-permute-done | bytes 688160 | tf_op jit(solution)/shard_map/ppermute | solution.py:33
  174.0 8.9 %collective-permute-start.19 = (bf16[4,6,16,256]{3,2,1,0:T(8,128)(2,1)S(1)}, bf16[4,6,16,256]{3,2,1,0:T(8,128)(2,1)S(1)}, u32[]{:S(2)}, u32[]{:S(2)}) collective-permute-start(bf16[4,6,16,256]{3,2,1,0:T(8,128)(2,1)S(1)} %get-tuple-element.48), channel_id=1, source_target_pairs={{0,64},{8,72},{16,80},{24,88},{32,96},{40,104},{48,112},{56,120},{... | collective-permute-start | bytes 589832 | tf_op jit(solution)/shard_map/ppermute | solution.py:42
  183.0 5.1 %collective-permute-start.21 = (bf16[4,6,16,256]{3,2,1,0:T(8,128)(2,1)S(1)}, bf16[4,6,16,256]{3,2,1,0:T(8,128)(2,1)S(1)}, u32[]{:S(2)}, u32[]{:S(2)}) collective-permute-start(bf16[4,6,16,256]{3,2,1,0:T(8,128)(2,1)S(1)} %get-tuple-element.50), channel_id=1, source_target_pairs={{0,128},{8,136},{16,144},{24,152},{32,160},{40,168},{48,176},{56,1... | collective-permute-start | bytes 589832 | tf_op jit(solution)/shard_map/ppermute | solution.py:42
  188.1 3.3 %collective-permute-start.26 = (bf16[4,5,16,256]{3,2,1,0:T(8,128)(2,1)S(1)}, bf16[4,5,16,256]{3,2,1,0:T(8,128)(2,1)S(1)}, u32[]{:S(2)}, u32[]{:S(2)}) collective-permute-start(bf16[4,5,16,256]{3,2,1,0:T(8,128)(2,1)S(1)} %get-tuple-element.57), channel_id=1, source_target_pairs={{0,48},{8,56},{16,0},{24,8},{32,16},{40,24},{48,32},{56,40},{64,11... | collective-permute-start | bytes 491528 | tf_op jit(solution)/shard_map/ppermute | solution.py:33
  191.4 4.0 %collective-permute-done.26.refs_6_ = bf16[4,5,16,256]{3,2,1,0:T(8,128)(2,1)S(1)} collective-permute-done((bf16[4,5,16,256]{3,2,1,0:T(8,128)(2,1)S(1)}, bf16[4,5,16,256]{3,2,1,0:T(8,128)(2,1)S(1)}, u32[]{:S(2)}, u32[]{:S(2)}) %collective-permute-start.26) | collective-permute-done | bytes 163872 | tf_op jit(solution)/shard_map/ppermute | solution.py:33
  197.8 4.5 %collective-permute-start.28 = (bf16[2,4,6,8,256]{4,3,2,1,0:T(8,128)(2,1)S(1)}, bf16[2,4,6,8,256]{4,3,2,1,0:T(8,128)(2,1)S(1)}, u32[]{:S(2)}, u32[]{:S(2)}) collective-permute-start(bf16[2,4,6,8,256]{4,3,2,1,0:T(8,128)(2,1)S(1)} %get-tuple-element.60), channel_id=1, source_target_pairs={{0,8},{8,0},{16,24},{24,16},{32,40},{40,32},{48,56},{56,48},{64,72... | collective-permute-start | bytes 589832 | tf_op jit(solution)/shard_map/ppermute | solution.py:37
  (113 shorter events, 45.8 us)
Async XLA Ops:
  7.2 41.9 %all-gather.3.cloned.1.call-start = ((), (), s32[]{:S(2)}) async-start(), calls=%async_computation.2 | async-start | bytes 2359296 | tf_op jit(solution)/shard_map/all_gather | solution.py:433
  8.9 195.9 %reduce-scatter.2.cloned.1.call-start = ((), (), s32[]{:S(2)}) async-start(), calls=%async_computation.1 | async-start | bytes 1179648 | tf_op jit(solution)/shard_map/reduce_scatter | solution.py:461
  13.3 16.3 %collective-permute-start.4 = (bf16[2,2,4,5,16,256]{5,4,3,2,1,0:T(8,128)(2,1)S(1)}, bf16[2,2,4,5,16,256]{5,4,3,2,1,0:T(8,128)(2,1)S(1)}, u32[]{:S(2)}, u32[]{:S(2)}) collective-permute-start(bf16[2,2,4,5,16,256]{5,4,3,2,1,0:T(8,128)(2,1)S(1)} %pad_maximum_fusion.refs_0_), channel_id=1, source_target_pairs={{0,48},{8,56},{16,0},{24,8},{32,16},{40,24},{48,32},{56,40},{64,11... | collective-permute-start | bytes 1966088 | tf_op jit(solution)/shard_map/ppermute | solution.py:33
  15.8 17.3 %collective-permute-start.1 = (bf16[2,2,4,5,16,256]{5,4,3,2,1,0:T(8,128)(2,1)S(1)}, bf16[2,2,4,5,16,256]{5,4,3,2,1,0:T(8,128)(2,1)S(1)}, u32[]{:S(2)}, u32[]{:S(2)}) collective-permute-start(bf16[2,2,4,5,16,256]{5,4,3,2,1,0:T(8,128)(2,1)S(1)} %pad_maximum_fusion.refs_0_), channel_id=1, source_target_pairs={{0,16},{8,24},{16,32},{24,40},{32,48},{40,56},{48,0},{56,8},{64,80... | collective-permute-start | bytes 1966088 | tf_op jit(solution)/shard_map/ppermute | solution.py:33
  29.6 9.3 %collective-permute-start.5 = (bf16[1,2,4,5,16,256]{5,4,3,2,1,0:T(8,128)(2,1)S(1)}, bf16[1,2,4,5,16,256]{5,4,3,2,1,0:T(8,128)(2,1)S(1)}, u32[]{:S(2)}, u32[]{:S(2)}) collective-permute-start(bf16[1,2,4,5,16,256]{5,4,3,2,1,0:T(8,128)(2,1)S(1)} %slice.9), channel_id=1, source_target_pairs={{0,48},{8,56},{16,0},{24,8},{32,16},{40,24},{48,32},{56,40},{64,11... | collective-permute-start | bytes 983048 | tf_op jit(solution)/shard_map/ppermute | solution.py:33
  33.1 9.0 %collective-permute-start.2 = (bf16[1,2,4,5,16,256]{5,4,3,2,1,0:T(8,128)(2,1)S(1)}, bf16[1,2,4,5,16,256]{5,4,3,2,1,0:T(8,128)(2,1)S(1)}, u32[]{:S(2)}, u32[]{:S(2)}) collective-permute-start(bf16[1,2,4,5,16,256]{5,4,3,2,1,0:T(8,128)(2,1)S(1)} %slice.8), channel_id=1, source_target_pairs={{0,16},{8,24},{16,32},{24,40},{32,48},{40,56},{48,0},{56,8},{64,80... | collective-permute-start | bytes 983048 | tf_op jit(solution)/shard_map/ppermute | solution.py:33
  49.8 33.7 %collective-permute-start.7 = (bf16[8,2,128,512]{3,2,1,0:T(8,128)(2,1)}, bf16[8,2,128,512]{3,2,1,0:T(8,128)(2,1)}, u32[]{:S(2)}, u32[]{:S(2)}) collective-permute-start(bf16[8,2,128,512]{3,2,1,0:T(8,128)(2,1)} %after.1.own), channel_id=1, source_target_pairs={{0,8},{8,0},{16,24},{24,16},{32,40},{40,32},{48,56},{56,48},{64,72... | collective-permute-start | bytes 6291464 | tf_op jit(solution)/shard_map/ppermute | solution.py:37
  53.0 16.4 %collective-permute-start.8 = (bf16[2,2,4,5,16,256]{5,4,3,2,1,0:T(8,128)(2,1)S(1)}, bf16[2,2,4,5,16,256]{5,4,3,2,1,0:T(8,128)(2,1)S(1)}, u32[]{:S(2)}, u32[]{:S(2)}) collective-permute-start(bf16[2,2,4,5,16,256]{5,4,3,2,1,0:T(8,128)(2,1)S(1)} %pad_maximum_fusion.refs_0_), channel_id=1, source_target_pairs={{0,64},{8,72},{16,80},{24,88},{32,96},{40,104},{48,112},{56,120},{... | collective-permute-start | bytes 1966088 | tf_op jit(solution)/shard_map/ppermute | solution.py:42
  54.3 16.2 %collective-permute-start.10 = (bf16[2,2,4,5,16,256]{5,4,3,2,1,0:T(8,128)(2,1)S(1)}, bf16[2,2,4,5,16,256]{5,4,3,2,1,0:T(8,128)(2,1)S(1)}, u32[]{:S(2)}, u32[]{:S(2)}) collective-permute-start(bf16[2,2,4,5,16,256]{5,4,3,2,1,0:T(8,128)(2,1)S(1)} %collective-permute-done.4.refs_2_), channel_id=1, source_target_pairs={{0,192},{8,200},{16,208},{24,216},{32,224},{40,232},{48,240},{56,2... | collective-permute-start | bytes 1966088 | tf_op jit(solution)/shard_map/ppermute | solution.py:42
  54.5 29.0 %collective-permute-start.9 = (bf16[2,2,4,5,16,256]{5,4,3,2,1,0:T(8,128)(2,1)S(1)}, bf16[2,2,4,5,16,256]{5,4,3,2,1,0:T(8,128)(2,1)}, u32[]{:S(2)}, u32[]{:S(2)}) collective-permute-start(bf16[2,2,4,5,16,256]{5,4,3,2,1,0:T(8,128)(2,1)S(1)} %collective-permute-done.1.refs_1_), channel_id=1, source_target_pairs={{0,64},{8,72},{16,80},{24,88},{32,96},{40,104},{48,112},{56,120},{... | collective-permute-start | bytes 1966088 | tf_op jit(solution)/shard_map/ppermute | solution.py:42
  92.2 12.1 %collective-permute-start.11 = (bf16[64,1024]{1,0:T(8,128)(2,1)S(1)}, bf16[64,1024]{1,0:T(8,128)(2,1)S(1)}, u32[]{:S(2)}, u32[]{:S(2)}) collective-permute-start(bf16[64,1024]{1,0:T(8,128)(2,1)S(1)} %get-tuple-element.35), channel_id=1, source_target_pairs={{0,16},{8,24},{16,32},{24,40},{32,48},{40,56},{48,64},{56,72},{64,... | collective-permute-start | bytes 393224 | tf_op jit(solution)/shard_map/ppermute | solution.py:50
  93.5 10.8 %collective-permute-start.12 = (bf16[64,1024]{1,0:T(8,128)(2,1)S(1)}, bf16[64,1024]{1,0:T(8,128)(2,1)S(1)}, u32[]{:S(2)}, u32[]{:S(2)}) collective-permute-start(bf16[64,1024]{1,0:T(8,128)(2,1)S(1)} %get-tuple-element.36), channel_id=1, source_target_pairs={{16,0},{24,8},{32,16},{40,24},{48,32},{56,40},{64,48},{72,56},{80,... | collective-permute-start | bytes 393224 | tf_op jit(solution)/shard_map/ppermute | solution.py:50
  98.8 12.7 %collective-permute-start.13 = (bf16[64,1024]{1,0:T(8,128)(2,1)S(1)}, bf16[64,1024]{1,0:T(8,128)(2,1)S(1)}, u32[]{:S(2)}, u32[]{:S(2)}) collective-permute-start(bf16[64,1024]{1,0:T(8,128)(2,1)S(1)} %get-tuple-element.40), channel_id=1, source_target_pairs={{0,16},{8,24},{16,32},{24,40},{32,48},{40,56},{48,64},{56,72},{64,... | collective-permute-start | bytes 393224 | tf_op jit(solution)/shard_map/ppermute | solution.py:50
  102.8 8.7 %collective-permute-start.14 = (bf16[64,1024]{1,0:T(8,128)(2,1)S(1)}, bf16[64,1024]{1,0:T(8,128)(2,1)S(1)}, u32[]{:S(2)}, u32[]{:S(2)}) collective-permute-start(bf16[64,1024]{1,0:T(8,128)(2,1)S(1)} %get-tuple-element.41), channel_id=1, source_target_pairs={{16,0},{24,8},{32,16},{40,24},{48,32},{56,40},{64,48},{72,56},{80,... | collective-permute-start | bytes 393224 | tf_op jit(solution)/shard_map/ppermute | solution.py:50
  129.2 25.2 %collective-permute-start.22 = (bf16[4,20,16,256]{3,2,1,0:T(8,128)(2,1)}, bf16[4,20,16,256]{3,2,1,0:T(8,128)(2,1)S(1)}, u32[]{:S(2)}, u32[]{:S(2)}) collective-permute-start(bf16[4,20,16,256]{3,2,1,0:T(8,128)(2,1)} %copy-done.24), channel_id=1, source_target_pairs={{0,64},{8,72},{16,80},{24,88},{32,96},{40,104},{48,112},{56,120},{... | collective-permute-start | bytes 1966088 | tf_op jit(solution)/shard_map/ppermute | solution.py:42
  137.9 16.4 %collective-permute-start.23 = (bf16[4,20,16,256]{3,2,1,0:T(8,128)(2,1)}, bf16[4,20,16,256]{3,2,1,0:T(8,128)(2,1)S(1)}, u32[]{:S(2)}, u32[]{:S(2)}) collective-permute-start(bf16[4,20,16,256]{3,2,1,0:T(8,128)(2,1)} %copy-done.23), channel_id=1, source_target_pairs={{0,192},{8,200},{16,208},{24,216},{32,224},{40,232},{48,240},{56,2... | collective-permute-start | bytes 1966088 | tf_op jit(solution)/shard_map/ppermute | solution.py:42
  139.3 29.8 %collective-permute-start.24 = (bf16[4,20,16,256]{3,2,1,0:T(8,128)(2,1)}, bf16[4,20,16,256]{3,2,1,0:T(8,128)(2,1)S(1)}, u32[]{:S(2)}, u32[]{:S(2)}) collective-permute-start(bf16[4,20,16,256]{3,2,1,0:T(8,128)(2,1)} %copy-done.22), channel_id=1, source_target_pairs={{0,128},{8,136},{16,144},{24,152},{32,160},{40,168},{48,176},{56,1... | collective-permute-start | bytes 1966088 | tf_op jit(solution)/shard_map/ppermute | solution.py:42
  140.4 29.8 %collective-permute-start.16 = (bf16[4,21,16,256]{3,2,1,0:T(8,128)(2,1)}, bf16[4,21,16,256]{3,2,1,0:T(8,128)(2,1)S(1)}, u32[]{:S(2)}, u32[]{:S(2)}) collective-permute-start(bf16[4,21,16,256]{3,2,1,0:T(8,128)(2,1)} %copy-done.21), channel_id=1, source_target_pairs={{0,16},{8,24},{16,32},{24,40},{32,48},{40,56},{48,0},{56,8},{64,80... | collective-permute-start | bytes 2064392 | tf_op jit(solution)/shard_map/ppermute | solution.py:33
  140.4 29.8 %collective-permute-start.17 = (bf16[4,21,16,256]{3,2,1,0:T(8,128)(2,1)S(1)}, bf16[4,21,16,256]{3,2,1,0:T(8,128)(2,1)S(1)}, u32[]{:S(2)}, u32[]{:S(2)}) collective-permute-start(bf16[4,21,16,256]{3,2,1,0:T(8,128)(2,1)S(1)} %get-tuple-element.45), channel_id=1, source_target_pairs={{0,48},{8,56},{16,0},{24,8},{32,16},{40,24},{48,32},{56,40},{64,11... | collective-permute-start | bytes 2064392 | tf_op jit(solution)/shard_map/ppermute | solution.py:33
  154.3 18.7 %collective-permute-start.18 = (bf16[4,21,16,256]{3,2,1,0:T(8,128)(2,1)S(1)}, bf16[4,21,16,256]{3,2,1,0:T(8,128)(2,1)S(1)}, u32[]{:S(2)}, u32[]{:S(2)}) collective-permute-start(bf16[4,21,16,256]{3,2,1,0:T(8,128)(2,1)S(1)} %copy-done.20), channel_id=1, source_target_pairs={{0,32},{8,40},{16,48},{24,56},{32,0},{40,8},{48,16},{56,24},{64,96... | collective-permute-start | bytes 2064392 | tf_op jit(solution)/shard_map/ppermute | solution.py:33
  170.1 21.3 %collective-permute-start.25 = (bf16[4,5,16,256]{3,2,1,0:T(8,128)(2,1)S(1)}, bf16[4,5,16,256]{3,2,1,0:T(8,128)(2,1)S(1)}, u32[]{:S(2)}, u32[]{:S(2)}) collective-permute-start(bf16[4,5,16,256]{3,2,1,0:T(8,128)(2,1)S(1)} %get-tuple-element.56), channel_id=1, source_target_pairs={{0,16},{8,24},{16,32},{24,40},{32,48},{40,56},{48,0},{56,8},{64,80... | collective-permute-start | bytes 491528 | tf_op jit(solution)/shard_map/ppermute | solution.py:33
  174.0 23.0 %collective-permute-start.19 = (bf16[4,6,16,256]{3,2,1,0:T(8,128)(2,1)S(1)}, bf16[4,6,16,256]{3,2,1,0:T(8,128)(2,1)S(1)}, u32[]{:S(2)}, u32[]{:S(2)}) collective-permute-start(bf16[4,6,16,256]{3,2,1,0:T(8,128)(2,1)S(1)} %get-tuple-element.48), channel_id=1, source_target_pairs={{0,64},{8,72},{16,80},{24,88},{32,96},{40,104},{48,112},{56,120},{... | collective-permute-start | bytes 589832 | tf_op jit(solution)/shard_map/ppermute | solution.py:42
  183.0 14.1 %collective-permute-start.20 = (bf16[4,6,16,256]{3,2,1,0:T(8,128)(2,1)S(1)}, bf16[4,6,16,256]{3,2,1,0:T(8,128)(2,1)S(1)}, u32[]{:S(2)}, u32[]{:S(2)}) collective-permute-start(bf16[4,6,16,256]{3,2,1,0:T(8,128)(2,1)S(1)} %get-tuple-element.49), channel_id=1, source_target_pairs={{0,192},{8,200},{16,208},{24,216},{32,224},{40,232},{48,240},{56,2... | collective-permute-start | bytes 589832 | tf_op jit(solution)/shard_map/ppermute | solution.py:42
  183.0 14.1 %collective-permute-start.21 = (bf16[4,6,16,256]{3,2,1,0:T(8,128)(2,1)S(1)}, bf16[4,6,16,256]{3,2,1,0:T(8,128)(2,1)S(1)}, u32[]{:S(2)}, u32[]{:S(2)}) collective-permute-start(bf16[4,6,16,256]{3,2,1,0:T(8,128)(2,1)S(1)} %get-tuple-element.50), channel_id=1, source_target_pairs={{0,128},{8,136},{16,144},{24,152},{32,160},{40,168},{48,176},{56,1... | collective-permute-start | bytes 589832 | tf_op jit(solution)/shard_map/ppermute | solution.py:42
  (32 other events, 336.0 us)
Sparse Core Ops, SparseCore 0:
  9.8 36.0 all-gather.2
  129.3 38.8 reduce-scatter.1
